TPU v7x, 32 devices: a whole 2x2x4 slice. The times are simulated.
32 devices in a mesh: crop: 2 (over y), rows: 4 (over x, core), hid: 4 (over z).
Axes of the slice: x: 2, y: 2, z: 4, core: 2. Of those that a mesh axis runs over, the one named last changes fastest.
Arguments:
- tokens: bfloat16 [2, 8, 64, 4096], P('crop', 'rows', None, 'hid'), may hold values from -6 to 6
- cotangent: bfloat16 [2, 8, 64, 4096], P('crop', 'rows', None, 'hid'), may hold values from -6 to 6
- weight_in: bfloat16 [256, 64, 5, 256], P('rows', 'hid'), may hold values from -0.15625 to 0.15625
- weight_out: bfloat16 [256, 64, 5, 256], P('rows', 'hid'), may hold values from -0.078125 to 0.078125
- mix_kernel: float32 [9, 16384], P(None, 'hid'), may hold values from -4 to 4
- block_rows: int32 [64, 5], P('hid'), may hold values from 0 to 15, as said below
Outputs:
- grad_tokens: bfloat16 [2, 8, 64, 4096], P('crop', 'rows', None, 'hid')
- grad_w_in: float32 [256, 64, 5, 256], P(('crop', 'rows'), 'hid')
- grad_w_out: float32 [256, 64, 5, 256], P(('crop', 'rows'), 'hid')
- grad_kernel: float32 [9, 16384], P(None, 'hid')
Inputs may be any that keep to these rules, and one draw needn't show every extreme that they name: In each block column c, block_rows[c, 0] is a label L and block_rows[c, k] for k >= 1 is L with bit k - 1 flipped, so the 5 entries of a column differ; every value is the label of equally many block columns.
All inputs are finite; a program needn't handle non-finite values.
Results may differ from a plain program's by a relative error of at most 0.019.
Values may be sent and summed in bfloat16 or wider, within the bound.
A program may use at most 128 MiB of HBM per device.

v0:
```python
import functools

import jax
import jax.numpy as jnp
from jax import lax
from jax.experimental import pallas as pl
from jax.experimental.pallas import tpu as pltpu
from jax.sharding import PartitionSpec as P

root_two_pi = 0.7978845608
cubic_coef = 0.044715
loss_scale = 0.03125

MESH_ID = pl.DeviceIdType.MESH
ANY = pl.BlockSpec(memory_space=pl.ANY)
VMEM = pl.BlockSpec(memory_space=pltpu.VMEM)
SMEM = pl.BlockSpec(memory_space=pltpu.SMEM)


def span(start, size):
    return pl.ds(pl.multiple_of(start * size, size), size)


def neighbours():
    y, r, z = lax.axis_index("crop"), lax.axis_index("rows"), lax.axis_index("hid")
    x, core = r // 2, r % 2
    same_chip = x * 2 + (1 - core)
    across = (1 - x) * 2 + core
    diagonal = (1 - x) * 2 + (1 - core)
    return y, r, z, same_chip, across, diagonal


def enter(partners):
    barrier = pltpu.get_barrier_semaphore()
    for partner in partners:
        pl.semaphore_signal(barrier, inc=1, device_id=partner, device_id_type=MESH_ID)
    pl.semaphore_wait(barrier, len(partners))


def remote(src, dst, send_sem, recv_sem, target):
    return pltpu.make_async_remote_copy(
        src_ref=src,
        dst_ref=dst,
        send_sem=send_sem,
        recv_sem=recv_sem,
        device_id=target,
        device_id_type=MESH_ID,
    )


def gather_kernel(
    depth, tok, cot, w_in, w_out, tok_all, cot_all, in_all, out_all,
    raw, flat, stage, tok_send, tok_recv, w_send, w_recv, own_sem, raw_sem,
):
    y, r, z, same_chip, across, diagonal = neighbours()
    tokens, features = tok.shape
    rows = w_in.shape[0]
    lanes = in_all.shape[1]
    half = rows // 2
    block = w_in.shape[2]
    all_cols = stage.shape[1] // rows
    nnz = w_in.shape[1] // all_cols
    loads = [
        pltpu.make_async_copy(src, raw.at[a], raw_sem.at[a]) for a, src in enumerate((w_in, w_out))
    ]
    for load in loads:
        load.start()
    enter(
        [{"rows": same_chip}, {"rows": across}, {"rows": diagonal}, {"crop": 1 - y}]
        + [{"hid": (z + step) % depth} for step in range(1, depth)]
    )
    streams = ((tok, tok_all), (cot, cot_all))
    panels = ((flat.at[0], in_all), (flat.at[1], out_all))
    targets = ({"hid": z + 1}, {"hid": z - 1}, {"rows": across}, {"rows": same_chip})
    has_up, has_down = z + 1 < depth, z >= 1
    sends, local = [], []

    def launch(make, have=None):
        sends.append((make, have))
        if have is None:
            make().start()
        else:
            pl.when(have)(lambda: make().start())

    def piece(full, row, col):
        return full.at[span(row, tokens), span(col, features)]

    def pass_on(a, which, col, kind, have=None, own=False):
        def make():
            row = (r, across)[which]
            part = piece(streams[a][1], row, col)
            return remote(
                streams[a][0] if own else part,
                part,
                tok_send.at[a, which, col, kind],
                tok_recv.at[a, row, col],
                targets[kind],
            )

        launch(make, have)

    def await_piece(a, row, col, have=None):
        def wait():
            part = piece(streams[a][1], row, col)
            remote(
                part, part, tok_send.at[a, 0, 0, 3], tok_recv.at[a, row, col], {"rows": same_chip}
            ).wait_recv()

        if have is None:
            wait()
        else:
            pl.when(have)(wait)

    def half_rows(full, row, h):
        return full.at[pl.ds(pl.multiple_of(row * rows + h * half, half), half), :]

    def flatten(a):
        def turn(k, carry):
            for h in range(block // 128):
                part = raw[a, :, span(k, all_cols), h * 128 : (h + 1) * 128]
                stage[h] = part.astype(jnp.float32).reshape(rows * all_cols, 128)
            for c in range(all_cols):
                for h in range(block // 128):
                    flat[a, :, pl.ds(pl.multiple_of((c * nnz + k) * block + h * 128, 128), 128)] = stage[
                        h, pl.ds(c, rows, stride=all_cols), :
                    ].astype(jnp.bfloat16)
            return carry

        lax.fori_loop(0, nnz, turn, 0)

    def give_weights(a):
        src, full = panels[a]
        loads[a].wait()
        flatten(a)
        for slot, dest in ((1, across), (2, diagonal)):
            launch(
                lambda slot=slot, dest=dest: remote(
                    src.at[span(y, half), span(dest, lanes)],
                    half_rows(full, r, y),
                    w_send.at[a, slot],
                    w_recv.at[a, r, y],
                    {"rows": dest},
                )
            )
        launch(
            lambda: remote(
                src.at[:, span(same_chip, lanes)],
                full.at[span(r, rows), :],
                w_send.at[a, 0],
                w_recv.at[a, r, 0],
                {"rows": same_chip},
            )
        )
        keep = pltpu.make_async_copy(
            src.at[:, span(r, lanes)], full.at[span(r, rows), :], own_sem.at[a, 1]
        )
        keep.start()
        local.append(keep)

    def mirror_weights(a):
        full = panels[a][1]
        for slot, row in ((3, across), (4, diagonal)):
            part = half_rows(full, row, y)
            remote(part, part, w_send.at[a, slot], w_recv.at[a, row, y], {"rows": row}).wait_recv()
            launch(
                lambda slot=slot, row=row, part=part: remote(
                    part, part, w_send.at[a, slot], w_recv.at[a, row, y], {"crop": 1 - y}
                )
            )

    def line_step(step):
        for below in (True, False):
            col = z - step if below else z + step
            have = col >= 0 if below else col < depth
            onward = jnp.logical_and(have, has_up if below else has_down)
            for a, which in ((0, 0), (1, 0), (1, 1)):
                await_piece(a, (r, across)[which], col, have)
                pass_on(a, which, col, 0 if below else 1, onward)
                if a == 0:
                    pass_on(a, which, col, 2, have)
                pass_on(a, which, col, 3, have)

    for a, kind in ((1, 2), (0, 0), (0, 1), (1, 0), (1, 1), (0, 2), (0, 3), (1, 3)):
        pass_on(a, 0, z, kind, (has_up, has_down, None, None)[kind], own=True)
    for a in range(2):
        keep = pltpu.make_async_copy(streams[a][0], piece(streams[a][1], r, z), own_sem.at[a, 0])
        keep.start()
        local.append(keep)
    give_weights(0)
    await_piece(1, across, z)
    for kind in (0, 1, 3):
        pass_on(1, 1, z, kind, (has_up, has_down, None, None)[kind])
    give_weights(1)
    for step in range(1, depth):
        line_step(step)
        if step <= 2:
            mirror_weights(step - 1)
    for a in range(depth - 1, 2):
        mirror_weights(a)
    for step in range(depth):
        col = (z + step) % depth
        await_piece(0, across, col)
        pass_on(0, 1, col, 3)
    for a in range(2):
        full = panels[a][1]
        part = full.at[span(same_chip, rows), :]
        remote(
            part, part, w_send.at[a, 0], w_recv.at[a, same_chip, 0], {"rows": same_chip}
        ).wait_recv()
        for row in (across, diagonal):
            part = half_rows(full, row, 1 - y)
            remote(
                part, part, w_send.at[a, 0], w_recv.at[a, row, 1 - y], {"crop": 1 - y}
            ).wait_recv()
        for row in (same_chip, diagonal):
            for step in range(depth):
                await_piece(a, row, (z + step) % depth)
    for copy in local:
        copy.wait()
    for make, have in sends:
        if have is None:
            make().wait_send()
        else:
            pl.when(have)(lambda make=make: make().wait_send())


def nt(a, b):
    return lax.dot_general(a, b, (((1,), (1,)), ((), ())), preferred_element_type=jnp.float32)


def tn(a, b):
    return lax.dot_general(a, b, (((0,), (0,)), ((), ())), preferred_element_type=jnp.float32)


def local_kernel(
    width, block, cols, nnz, ids, tok, cot, w_in, w_out, taps,
    dx_out, gw_in, gw_out, kern_out, kern, dx, pre_s, act_s, slope_s, mg_s,
):
    count = tok.shape[0]
    me = lax.axis_index("rows")
    c = pl.program_id(0)
    place = lax.broadcasted_iota(jnp.int32, (count, block), 0) % width

    @pl.when(c == 0)
    def _():
        dx[...] = jnp.zeros_like(dx)
        kern[...] = jnp.zeros_like(kern)

    def spread(value):
        before = jnp.where(place == 0, 0.0, pltpu.roll(value, 1, 0))
        after = jnp.where(place == width - 1, 0.0, pltpu.roll(value, count - 1, 0))
        return (before, value, after)

    def stack_rows(up, mid, down):
        edge = jnp.zeros((width, block), jnp.float32)
        return (
            mid
            + jnp.concatenate([edge, up[:-width]], axis=0)
            + jnp.concatenate([down[width:], edge], axis=0)
        )

    hidden = span(c, block)

    def feats(k):
        return span(ids[k, me * cols + c], block)

    def panel(k):
        return slice(k * block, (k + 1) * block)

    pre = jnp.dot(tok[:, feats(0)], w_in[:, panel(0)], preferred_element_type=jnp.float32)
    for k in range(1, nnz):
        pre += jnp.dot(tok[:, feats(k)], w_in[:, panel(k)], preferred_element_type=jnp.float32)
    pre_s[...] = pre
    mg = nt(cot[:, feats(0)], w_out[:, panel(0)])
    for k in range(1, nnz):
        mg += nt(cot[:, feats(k)], w_out[:, panel(k)])
    mg_s[...] = mg.astype(jnp.bfloat16).astype(jnp.float32)
    p = pre_s[...]
    t = jnp.tanh(root_two_pi * (p + cubic_coef * p * p * p))
    act_s[...] = (0.5 * p * (1.0 + t)).astype(jnp.bfloat16).astype(jnp.float32)
    slope_s[...] = 0.5 * (1.0 + t) + 0.5 * p * (1.0 - t * t) * root_two_pi * (
        1.0 + 3.0 * cubic_coef * p * p
    )

    def tap(a, b):
        row = 3 * (a + 1) + (b + 1)
        return taps[row : row + 1, span(me * cols + c, block)]

    acts = spread(act_s[...])
    mixed = stack_rows(
        *[sum(tap(a, b) * acts[b + 1] for b in (-1, 0, 1)) for a in (-1, 0, 1)]
    ).astype(jnp.bfloat16)
    grads = mg_s[...]
    for b in (-1, 0, 1):
        seen = acts[b + 1]
        sums = (
            jnp.sum(seen[:-width] * grads[width:], axis=0, keepdims=True),
            jnp.sum(seen * grads, axis=0, keepdims=True),
            jnp.sum(seen[width:] * grads[:-width], axis=0, keepdims=True),
        )
        for a in (-1, 0, 1):
            row = 3 * (a + 1) + (b + 1)
            kern[row : row + 1, hidden] = sums[a + 1] * loss_scale
    for k in range(nnz):
        gw_out[:, panel(k)] = (tn(mixed, cot[:, feats(k)]) * loss_scale).astype(jnp.bfloat16)
    backs = spread(mg_s[...])
    gathered = stack_rows(
        *[sum(tap(a, b) * backs[1 - b] for b in (-1, 0, 1)) for a in (1, 0, -1)]
    )
    pre_grad = (gathered * slope_s[...]).astype(jnp.bfloat16)
    for k in range(nnz):
        gw_in[:, panel(k)] = (tn(tok[:, feats(k)], pre_grad) * loss_scale).astype(jnp.bfloat16)
        dx[:, feats(k)] += nt(pre_grad, w_in[:, panel(k)])

    @pl.when(c == cols - 1)
    def _():
        dx_out[...] = dx[...].astype(jnp.bfloat16)
        kern_out[...] = kern[...].astype(jnp.bfloat16)


def scatter_kernel(
    depth, dx, gw_in, gw_out, kern, dx_mine, in_mine, out_mine, kern_all,
    dx_own, gw_own, dx_near, dx_half, dx_far, dx_sum, dx_last, gw_part, gw_sum, kern_part,
    dx_send, dx_recv, gw_send, gw_recv, kern_send, kern_recv, dx_load, gw_load,
):
    y, r, z, same_chip, across, diagonal = neighbours()
    group = [same_chip, across, diagonal]
    order = (across, diagonal, same_chip, r)
    tokens, features = dx_mine.shape
    rows = in_mine.shape[0]
    lanes = gw_in.shape[1]
    weights = ((gw_in, in_mine), (gw_out, out_mine))
    enter(
        [{"rows": row} for row in group]
        + [{"crop": 1 - y}]
        + [{"hid": (z + step) % depth} for step in range(1, depth)]
    )
    started = []

    def go(*args):
        copy = remote(*args)
        copy.start()
        started.append(copy)

    go(kern, kern_part.at[1, 0], kern_send.at[0], kern_recv.at[1, 0], {"crop": 1 - y})
    for slot, row in enumerate((diagonal, same_chip)):
        go(dx.at[span(row, tokens), :], dx_near.at[slot], dx_send.at[slot], dx_recv.at[slot], {"rows": same_chip})
    for slot, row in enumerate(order):
        for a in range(2):
            go(
                weights[a][0].at[span((1 - y) * 4 + row, rows), :],
                gw_part.at[a, slot],
                gw_send.at[a, slot],
                gw_recv.at[a, slot],
                {"crop": 1 - y},
            )
    dx_loads = [
        pltpu.make_async_copy(dx.at[span(row, tokens), :], dx_own.at[slot], dx_load.at[slot])
        for slot, row in enumerate((across, r))
    ]
    gw_loads = [
        [
            pltpu.make_async_copy(
                weights[a][0].at[span(y * 4 + row, rows), :], gw_own.at[a, slot], gw_load.at[a, slot]
            )
            for a in range(2)
        ]
        for slot, row in enumerate(order)
    ]
    for load in dx_loads + [load for pair in gw_loads for load in pair]:
        load.start()
    def arrived(ref, send_sem, recv_sem, target):
        remote(ref, ref, send_sem, recv_sem, target).wait_recv()

    arrived(dx_near.at[0], dx_send.at[0], dx_recv.at[0], {"rows": same_chip})
    dx_loads[0].wait()
    dx_half[...] = (
        dx_own[0].astype(jnp.float32) + dx_near[0].astype(jnp.float32)
    ).astype(jnp.bfloat16)
    arrived(kern_part.at[1, 0], kern_send.at[0], kern_recv.at[1, 0], {"crop": 1 - y})
    kern_part[0, r] = (
        kern[...].astype(jnp.float32) + kern_part[1, 0].astype(jnp.float32)
    ).astype(jnp.bfloat16)
    for slot, row in enumerate(group):
        go(
            kern_part.at[0, r],
            kern_part.at[0, r],
            kern_send.at[slot + 1],
            kern_recv.at[0, r],
            {"rows": row},
        )
    go(dx_half, dx_far, dx_send.at[2], dx_recv.at[2], {"rows": across})
    arrived(dx_near.at[1], dx_send.at[1], dx_recv.at[1], {"rows": same_chip})
    arrived(dx_far, dx_send.at[2], dx_recv.at[2], {"rows": across})
    dx_loads[1].wait()
    for col in range(depth):
        part = slice(col * features, (col + 1) * features)
        dx_sum[col] = (
            dx_own[1, :, part].astype(jnp.float32)
            + dx_near[1, :, part].astype(jnp.float32)
            + dx_far[:, part].astype(jnp.float32)
        ).astype(jnp.bfloat16)
    for step in range(1, depth):
        go(
            dx_sum.at[(z + step) % depth],
            dx_last.at[step - 1],
            dx_send.at[2 + step],
            dx_recv.at[2 + step],
            {"hid": (z + step) % depth},
        )
    for slot, row in enumerate(order):
        for a in range(2):
            arrived(gw_part.at[a, slot], gw_send.at[a, slot], gw_recv.at[a, slot], {"crop": 1 - y})
            gw_loads[slot][a].wait()
            total = (
                gw_own[a, slot].astype(jnp.float32)
                + gw_part[a, slot].astype(jnp.float32)
            ).astype(jnp.bfloat16)
            if slot == 3:
                weights[a][1][:, span(r, lanes)] = total
            else:
                gw_sum[a, slot] = total
                go(
                    gw_sum.at[a, slot],
                    weights[a][1].at[:, span(r, lanes)],
                    gw_send.at[a, 4 + slot],
                    gw_recv.at[a, 4 + slot],
                    {"rows": row},
                )
    total = dx_sum[z].astype(jnp.float32)
    for step in range(1, depth):
        arrived(dx_last.at[step - 1], dx_send.at[2 + step], dx_recv.at[2 + step], {"hid": (z + step) % depth})
        total += dx_last[step - 1].astype(jnp.float32)
    dx_mine[...] = total.astype(jnp.bfloat16)
    for row in group:
        arrived(kern_part.at[0, row], kern_send.at[0], kern_recv.at[0, row], {"rows": same_chip})
    wide = kern.shape[1]
    for row in range(4):
        kern_all[:, row * wide : (row + 1) * wide] = kern_part[0, row].astype(jnp.float32)
    for slot, row in enumerate(order[:3]):
        for a in range(2):
            arrived(
                weights[a][1].at[:, span(row, lanes)],
                gw_send.at[a, 4 + slot],
                gw_recv.at[a, 4 + slot],
                {"rows": row},
            )
    for copy in started:
        copy.wait_send()


def finish_kernel(
    all_cols, nnz, in_mine, out_mine, dx_mine, kern_all, in_grad, out_grad, dx_grad, kern_grad
):
    block = in_grad.shape[2]
    dx_grad[...] = dx_mine[...]
    kern_grad[...] = kern_all[: kern_grad.shape[0]]
    for src, dst in ((in_mine, in_grad), (out_mine, out_grad)):
        for c in range(all_cols):
            for k in range(nnz):
                at = (c * nnz + k) * block
                dst[:, k * all_cols + c, :] = src[:, at : at + block].astype(jnp.float32)


def split_hidden(tokens, cotangent, weight_in, weight_out, mix_kernel, block_rows):
    n_rows, depth = lax.axis_size("rows"), lax.axis_size("hid")
    _, height, width, features = tokens.shape
    rows, all_cols, nnz, block = weight_in.shape
    count = height * width
    whole = count * n_rows
    model = features * depth
    cols = all_cols // n_rows
    lanes = cols * nnz * block
    hidden = cols * block
    bf16, f32 = jnp.bfloat16, jnp.float32
    dma, sds = pltpu.SemaphoreType.DMA, jax.ShapeDtypeStruct
    params = functools.partial(pltpu.CompilerParams, vmem_limit_bytes=60 * 1024 * 1024)
    tok_all, cot_all, in_all, out_all = pl.pallas_call(
        functools.partial(gather_kernel, depth),
        name="gather_parts",
        out_shape=[sds((whole, model), bf16)] * 2 + [sds((rows * n_rows, lanes), bf16)] * 2,
        in_specs=[ANY] * 4,
        out_specs=[ANY] * 4,
        scratch_shapes=[
            pltpu.VMEM((2, rows, nnz * all_cols, block), bf16),
            pltpu.VMEM((2, rows, all_cols * nnz * block), bf16),
            pltpu.VMEM((block // 128, rows * all_cols, 128), f32),
            dma((2, 2, depth, 4)),
            dma((2, n_rows, depth)),
            dma((2, 5)),
            dma((2, n_rows, 2)),
            dma((2, 2)),
            dma((2,)),
        ],
        compiler_params=params(collective_id=1, has_side_effects=True),
    )(
        tokens.reshape(count, features),
        cotangent.reshape(count, features),
        weight_in.transpose(0, 2, 1, 3).reshape(rows, nnz * all_cols, block),
        weight_out.transpose(0, 2, 1, 3).reshape(rows, nnz * all_cols, block),
    )
    panel_spec = pl.BlockSpec((block, nnz * block), lambda c: (0, c))
    dx, gw_in, gw_out, kern = pl.pallas_call(
        functools.partial(local_kernel, width, block, cols, nnz),
        name="local_math",
        out_shape=[
            sds((whole, model), bf16),
            sds((block, lanes), bf16),
            sds((block, lanes), bf16),
            sds((16, hidden), bf16),
        ],
        grid=(cols,),
        in_specs=[SMEM, VMEM, VMEM, panel_spec, panel_spec, VMEM],
        out_specs=[VMEM, panel_spec, panel_spec, VMEM],
        scratch_shapes=[pltpu.VMEM((16, hidden), f32), pltpu.VMEM((whole, model), f32)]
        + [pltpu.VMEM((whole, block), f32)] * 4,
        compiler_params=params(),
    )(block_rows.T, tok_all, cot_all, in_all, out_all, mix_kernel)
    out_rows = block // (n_rows * lax.axis_size("crop"))
    dx_mine, in_mine, out_mine, kern_all = pl.pallas_call(
        functools.partial(scatter_kernel, depth),
        name="scatter_sums",
        out_shape=[
            sds((count, features), bf16),
            sds((out_rows, all_cols * nnz * block), bf16),
            sds((out_rows, all_cols * nnz * block), bf16),
            sds((16, hidden * n_rows), f32),
        ],
        in_specs=[ANY] * 3 + [VMEM],
        out_specs=[VMEM] * 4,
        scratch_shapes=[
            pltpu.VMEM((2, count, model), bf16),
            pltpu.VMEM((2, 4, out_rows, lanes), bf16),
            pltpu.VMEM((2, count, model), bf16),
            pltpu.VMEM((count, model), bf16),
            pltpu.VMEM((count, model), bf16),
            pltpu.VMEM((depth, count, features), bf16),
            pltpu.VMEM((depth - 1, count, features), bf16),
            pltpu.VMEM((2, 4, out_rows, lanes), bf16),
            pltpu.VMEM((2, 3, out_rows, lanes), bf16),
            pltpu.VMEM((2, n_rows, 16, hidden), bf16),
            dma((2 + depth,)),
            dma((2 + depth,)),
            dma((2, 7)),
            dma((2, 7)),
            dma((4,)),
            dma((2, n_rows)),
            dma((2,)),
            dma((2, 4)),
        ],
        compiler_params=params(collective_id=2, has_side_effects=True),
    )(dx, gw_in, gw_out, kern)
    step = 8
    part = pl.BlockSpec((count * step // out_rows, features), lambda i: (i, 0))
    flat_spec = pl.BlockSpec((step, all_cols * nnz * block), lambda i: (i, 0))
    grad_spec = pl.BlockSpec((step, nnz * all_cols, block), lambda i: (i, 0, 0))
    in_grad, out_grad, dx_grad, kern_grad = pl.pallas_call(
        functools.partial(finish_kernel, all_cols, nnz),
        name="finish_weights",
        grid=(out_rows // step,),
        out_shape=[sds((out_rows, nnz * all_cols, block), f32)] * 2
        + [sds((count, features), bf16), sds(mix_kernel.shape, f32)],
        in_specs=[flat_spec] * 2 + [part, VMEM],
        out_specs=[grad_spec] * 2 + [part, VMEM],
        compiler_params=params(),
    )(in_mine, out_mine, dx_mine, kern_all)
    in_grad, out_grad = [
        grad.reshape(out_rows, nnz, all_cols, block).transpose(0, 2, 1, 3) for grad in (in_grad, out_grad)
    ]
    return (dx_grad.reshape(tokens.shape), in_grad, out_grad, kern_grad)


def padded(shard, sides, width):
    for axis, dim in sides:
        devices, length = (lax.axis_size(axis), shard.shape[dim])
        up = [(i, (i + 1) % devices) for i in range(devices - 1)]
        down = [(j, i) for i, j in up]
        last = lax.slice_in_dim(shard, length - width, length, axis=dim)
        initial = lax.slice_in_dim(shard, 0, width, axis=dim)
        before = lax.ppermute(last, axis, up)
        after = lax.ppermute(initial, axis, down)
        shard = jnp.concatenate([before, shard, after], axis=dim)
    return shard


def gelu_pair(preact):
    inner = root_two_pi * (preact + cubic_coef * preact * preact * preact)
    tanh_val = jnp.tanh(inner)
    gelu_out = 0.5 * preact * (1.0 + tanh_val)
    slopes = 0.5 * (1.0 + tanh_val) + 0.5 * preact * (1.0 - tanh_val * tanh_val) * root_two_pi * (
        1.0 + 3.0 * cubic_coef * preact * preact
    )
    return (gelu_out, slopes)


def on_device(tokens, cotangent, weight_in, weight_out, mix_kernel, block_rows):
    in_panel, out_panel = (
        lax.all_gather(weight_in, "rows", axis=0, tiled=True),
        lax.all_gather(weight_out, "rows", axis=0, tiled=True),
    )
    tok_full, cot_full = (
        lax.all_gather(tokens, "hid", axis=3, tiled=True),
        lax.all_gather(cotangent, "hid", axis=3, tiled=True),
    )
    crop_count, height, grid_width, depth_all = tok_full.shape
    tok_count = crop_count * height * grid_width
    block_size = in_panel.shape[0]
    col_count = in_panel.shape[1]
    nnz_count = in_panel.shape[2]
    block_count = depth_all // block_size
    hidden_local = col_count * block_size
    flat_rows = block_rows.reshape(-1)
    in_select = jnp.take(
        tok_full.reshape(tok_count, block_count, block_size), flat_rows, axis=1
    ).reshape(tok_count, col_count, nnz_count, block_size)
    grad_select = jnp.take(
        cot_full.reshape(tok_count, block_count, block_size), flat_rows, axis=1
    ).reshape(tok_count, col_count, nnz_count, block_size)
    pre_act = jnp.einsum("tckb,bcke->tce", in_select, in_panel, preferred_element_type=jnp.float32)
    gelu_out, slopes = gelu_pair(pre_act)
    active = gelu_out.astype(jnp.bfloat16).reshape(crop_count, height, grid_width, hidden_local)
    act_rim = padded(active, (("rows", 1),), 1)
    mix_grad = (
        jnp.einsum("tckd,fckd->tcf", grad_select, out_panel, preferred_element_type=jnp.float32)
        .astype(jnp.bfloat16)
        .reshape(crop_count, height, grid_width, hidden_local)
    )
    grad_rim = padded(mix_grad, (("rows", 1),), 1)
    act_pad = jnp.pad(act_rim.astype(jnp.float32), ((0, 0), (0, 0), (1, 1), (0, 0)))
    grad_pad = jnp.pad(grad_rim.astype(jnp.float32), ((0, 0), (0, 0), (1, 1), (0, 0)))
    grad_grid = mix_grad.astype(jnp.float32)
    mix_sum = jnp.zeros((crop_count, height, grid_width, hidden_local), jnp.float32)
    act_grad = jnp.zeros((crop_count, height, grid_width, hidden_local), jnp.float32)
    kern_terms = []
    for row_off in range(3):
        for col_off in range(3):
            tap = mix_kernel[3 * row_off + col_off]
            shifted = act_pad[:, row_off : row_off + height, col_off : col_off + grid_width]
            mix_sum = mix_sum + tap * shifted
            act_grad = (
                act_grad
                + tap
                * grad_pad[
                    :, 2 - row_off : 2 - row_off + height, 2 - col_off : 2 - col_off + grid_width
                ]
            )
            kern_terms.append(jnp.sum(shifted * grad_grid, axis=(0, 1, 2)))
    kern_local = jnp.stack(kern_terms, axis=0) * loss_scale
    mix_out = mix_sum.astype(jnp.bfloat16).reshape(tok_count, col_count, block_size)
    pre_grad = (act_grad.reshape(tok_count, col_count, block_size) * slopes).astype(jnp.bfloat16)
    kern_total = lax.psum(kern_local.astype(jnp.bfloat16), ("crop", "rows")).astype(jnp.float32)
    back_select = jnp.einsum(
        "tce,bcke->tckb", pre_grad, in_panel, preferred_element_type=jnp.float32
    )
    one_hot = (
        block_rows[:, :, None] == jnp.arange(block_count, dtype=jnp.int32)[None, None, :]
    ).astype(jnp.float32)
    token_terms = jnp.einsum(
        "tckb,ckr->trb", back_select, one_hot, precision=lax.Precision.HIGHEST
    ).reshape(crop_count, height, grid_width, depth_all)
    grad_tokens = lax.psum_scatter(
        token_terms.astype(jnp.bfloat16), "hid", scatter_dimension=3, tiled=True
    )
    first_term = jnp.einsum(
        "tckb,tce->bcke", in_select, pre_grad, preferred_element_type=jnp.float32
    )
    second_term = jnp.einsum(
        "tcf,tckd->fckd", mix_out, grad_select, preferred_element_type=jnp.float32
    )
    share_sums = lax.psum_scatter(
        (jnp.stack([first_term, second_term], axis=1) * loss_scale).astype(jnp.bfloat16),
        ("crop", "rows"),
        scatter_dimension=0,
        tiled=True,
    ).astype(jnp.float32)
    return (grad_tokens, share_sums[:, 0], share_sums[:, 1], kern_total)


def solution(mesh):
    placed = (
        P("crop", "rows", None, "hid"),
        P("crop", "rows", None, "hid"),
        P("rows", "hid", None, None),
        P("rows", "hid", None, None),
        P(None, "hid"),
        P("hid", None),
    )
    n_crop, n_rows = mesh.shape["crop"], mesh.shape["rows"]
    n_hid = mesh.shape["hid"]

    def step(tokens, cotangent, weight_in, weight_out, mix_kernel, block_rows):
        fits = (
            n_crop == 2
            and n_rows == 4
            and tokens.shape[0] == 1
            and weight_in.shape[1] % n_rows == 0
            and tokens.shape[1] * tokens.shape[2] * n_rows * tokens.shape[3] * n_hid <= 2**22
        )
        chosen = split_hidden if fits else on_device
        return chosen(tokens, cotangent, weight_in, weight_out, mix_kernel, block_rows)

    return jax.shard_map(
        step,
        mesh=mesh,
        in_specs=placed,
        out_specs=(
            P("crop", "rows", None, "hid"),
            P(("crop", "rows"), "hid", None, None),
            P(("crop", "rows"), "hid", None, None),
            P(None, "hid"),
        ),
        check_vma=False,
    )
```

profile of v0, /device:TPU:0, one launch (start us, length us, event | category | flops | bytes accessed | tf_op | source)
XLA Modules:
  0.0 158.2 jit_solution(17631144969017572538)
XLA Ops:
  0.6 66.2 %gather_parts.1 = (bf16[512,4096]{1,0:T(8,128)(2,1)}, bf16[512,4096]{1,0:T(8,128)(2,1)}, bf16[256,5120]{1,0:T(8,128)(2,1)}, bf16[256,5120]{1,0:T(8,128)(2,1)}) custom-call(bf16[128,1024]{1,0:T(8,128)(2,1)} %bitcast.18, bf16[128,1024]{1,0:T(8,128)(2,1)} %bitcast.19, bf16[64,80,256]{2,1,0:T(8,128)(2,1)} %bitcast.16, bf16[64,80,256]{2,1,0:T(8,128)(2,1)} %bitcast.17), custom_call_target="tpu_custom_call" | custom-call | tf_op jit(solution)/shard_map/gather_parts/pallas_call | solution.py:478
  66.8 20.7 %local_math.1 = (bf16[512,4096]{1,0:T(8,128)(2,1)}, bf16[256,5120]{1,0:T(8,128)(2,1)}, bf16[256,5120]{1,0:T(8,128)(2,1)}, bf16[16,1024]{1,0:T(8,128)(2,1)}) custom-call(s32[5,16]{1,0:T(8,128)} %bitcast.20, bf16[512,4096]{1,0:T(8,128)(2,1)} %get-tuple-element.20.tok, bf16[512,4096]{1,0:T(8,128)(2,1)} %get-tuple-element.21.cot, ...), custom_call_target="tpu_custom_call" | custom-call | tf_op jit(solution)/shard_map/local_math/pallas_call | solution.py:503
  87.6 64.7 %scatter_sums.1 = (bf16[128,1024]{1,0:T(8,128)(2,1)}, bf16[32,20480]{1,0:T(8,128)(2,1)}, bf16[32,20480]{1,0:T(8,128)(2,1)}, f32[16,4096]{1,0:T(8,128)}) custom-call(bf16[512,4096]{1,0:T(8,128)(2,1)} %get-tuple-element.24.dx, bf16[256,5120]{1,0:T(8,128)(2,1)} %get-tuple-element.25.gw_in, bf16[256,5120]{1,0:T(8,128)(2,1)} %get-tuple-element.26.gw_out, ...), custom_call_target="tpu_custom_call" | custom-call | tf_op jit(solution)/shard_map/scatter_sums/pallas_call | solution.py:520
  152.3 5.9 %finish_weights.1 = (f32[32,80,256]{2,1,0:T(8,128)}, f32[32,80,256]{2,1,0:T(8,128)}, bf16[128,1024]{1,0:T(8,128)(2,1)}, f32[9,4096]{1,0:T(8,128)}) custom-call(bf16[32,20480]{1,0:T(8,128)(2,1)} %get-tuple-element.28.in_mine, bf16[32,20480]{1,0:T(8,128)(2,1)} %get-tuple-element.29.out_mine, bf16[128,1024]{1,0:T(8,128)(2,1)} %get-tuple-element.30.dx_mine, ...), custom_call_target="tpu_custom_call" | custom-call | tf_op jit(solution)/shard_map/finish_weights/pallas_call | solution.py:557
where the time goes:
time: 158 us
  Pallas kernels  158 us (100%)
    pallas_call x1, Pallas kernels, split_hidden(): pl.pallas_call(functools.partial(gather_kernel, depth), name='gather_part...  66.2 us
    pallas_call x1, Pallas kernels, split_hidden(): pl.pallas_call(functools.partial(scatter_kernel, depth), name='scatter_su...  64.7 us
    pallas_call x1, Pallas kernels, split_hidden(): pl.pallas_call(functools.partial(local_kernel, width, block, cols, nnz),...  20.7 us
    pallas_call x1, Pallas kernels, split_hidden(): pl.pallas_call(functools.partial(finish_kernel, all_cols, nnz), name='fin...  5.91 us

commit v1 on v0

--- a/solution.py
+++ b/solution.py
@@ -232,19 +232,10 @@
     return lax.dot_general(a, b, (((0,), (0,)), ((), ())), preferred_element_type=jnp.float32)
 
 
-def local_kernel(
-    width, block, cols, nnz, ids, tok, cot, w_in, w_out, taps,
-    dx_out, gw_in, gw_out, kern_out, kern, dx, pre_s, act_s, slope_s, mg_s,
-):
-    count = tok.shape[0]
+def column_math(width, block, cols, nnz, ids, tok, cot, w_in, w_out, taps, kern, mixed, pgrad, pre_s, act_s, slope_s, mg_s, gw):
+    count = tok.shape[1]
     me = lax.axis_index("rows")
-    c = pl.program_id(0)
     place = lax.broadcasted_iota(jnp.int32, (count, block), 0) % width
-
-    @pl.when(c == 0)
-    def _():
-        dx[...] = jnp.zeros_like(dx)
-        kern[...] = jnp.zeros_like(kern)
 
     def spread(value):
         before = jnp.where(place == 0, 0.0, pltpu.roll(value, 1, 0))
@@ -259,77 +250,118 @@
             + jnp.concatenate([down[width:], edge], axis=0)
         )
 
-    hidden = span(c, block)
-
-    def feats(k):
-        return span(ids[k, me * cols + c], block)
-
-    def panel(k):
-        return slice(k * block, (k + 1) * block)
-
-    pre = jnp.dot(tok[:, feats(0)], w_in[:, panel(0)], preferred_element_type=jnp.float32)
-    for k in range(1, nnz):
-        pre += jnp.dot(tok[:, feats(k)], w_in[:, panel(k)], preferred_element_type=jnp.float32)
-    pre_s[...] = pre
-    mg = nt(cot[:, feats(0)], w_out[:, panel(0)])
-    for k in range(1, nnz):
-        mg += nt(cot[:, feats(k)], w_out[:, panel(k)])
-    mg_s[...] = mg.astype(jnp.bfloat16).astype(jnp.float32)
-    p = pre_s[...]
-    t = jnp.tanh(root_two_pi * (p + cubic_coef * p * p * p))
-    act_s[...] = (0.5 * p * (1.0 + t)).astype(jnp.bfloat16).astype(jnp.float32)
-    slope_s[...] = 0.5 * (1.0 + t) + 0.5 * p * (1.0 - t * t) * root_two_pi * (
-        1.0 + 3.0 * cubic_coef * p * p
-    )
-
-    def tap(a, b):
+    def feats(c, k):
+        return ids[k, me * cols + c]
+
+    def panel(c, k):
+        return span(c * nnz + k, block)
+
+    def tap(c, a, b):
         row = 3 * (a + 1) + (b + 1)
         return taps[row : row + 1, span(me * cols + c, block)]
 
-    acts = spread(act_s[...])
-    mixed = stack_rows(
-        *[sum(tap(a, b) * acts[b + 1] for b in (-1, 0, 1)) for a in (-1, 0, 1)]
-    ).astype(jnp.bfloat16)
-    grads = mg_s[...]
-    for b in (-1, 0, 1):
-        seen = acts[b + 1]
-        sums = (
-            jnp.sum(seen[:-width] * grads[width:], axis=0, keepdims=True),
-            jnp.sum(seen * grads, axis=0, keepdims=True),
-            jnp.sum(seen[width:] * grads[:-width], axis=0, keepdims=True),
+    def forward(c, ready=None):
+        hidden = span(c, block)
+        pre = jnp.dot(tok[feats(c, 0)], w_in[c * nnz], preferred_element_type=jnp.float32)
+        for k in range(1, nnz):
+            pre += jnp.dot(tok[feats(c, k)], w_in[c * nnz + k], preferred_element_type=jnp.float32)
+        pre_s[...] = pre
+        p = pre_s[...]
+        t = jnp.tanh(root_two_pi * (p + cubic_coef * p * p * p))
+        act_s[...] = (0.5 * p * (1.0 + t)).astype(jnp.bfloat16).astype(jnp.float32)
+        slope_s[...] = 0.5 * (1.0 + t) + 0.5 * p * (1.0 - t * t) * root_two_pi * (
+            1.0 + 3.0 * cubic_coef * p * p
         )
-        for a in (-1, 0, 1):
-            row = 3 * (a + 1) + (b + 1)
-            kern[row : row + 1, hidden] = sums[a + 1] * loss_scale
-    for k in range(nnz):
-        gw_out[:, panel(k)] = (tn(mixed, cot[:, feats(k)]) * loss_scale).astype(jnp.bfloat16)
-    backs = spread(mg_s[...])
-    gathered = stack_rows(
-        *[sum(tap(a, b) * backs[1 - b] for b in (-1, 0, 1)) for a in (1, 0, -1)]
-    )
-    pre_grad = (gathered * slope_s[...]).astype(jnp.bfloat16)
-    for k in range(nnz):
-        gw_in[:, panel(k)] = (tn(tok[:, feats(k)], pre_grad) * loss_scale).astype(jnp.bfloat16)
-        dx[:, feats(k)] += nt(pre_grad, w_in[:, panel(k)])
-
-    @pl.when(c == cols - 1)
-    def _():
-        dx_out[...] = dx[...].astype(jnp.bfloat16)
-        kern_out[...] = kern[...].astype(jnp.bfloat16)
-
-
-def scatter_kernel(
-    depth, dx, gw_in, gw_out, kern, dx_mine, in_mine, out_mine, kern_all,
-    dx_own, gw_own, dx_near, dx_half, dx_far, dx_sum, dx_last, gw_part, gw_sum, kern_part,
-    dx_send, dx_recv, gw_send, gw_recv, kern_send, kern_recv, dx_load, gw_load,
+        acts = spread(act_s[...])
+        mixed[:, hidden] = stack_rows(
+            *[sum(tap(c, a, b) * acts[b + 1] for b in (-1, 0, 1)) for a in (-1, 0, 1)]
+        ).astype(jnp.bfloat16)
+        if ready is not None:
+            ready()
+
+    def backward(c):
+        hidden = span(c, block)
+        mg = nt(cot[feats(c, 0)], w_out[:, panel(c, 0)])
+        for k in range(1, nnz):
+            mg += nt(cot[feats(c, k)], w_out[:, panel(c, k)])
+        mg_s[...] = mg.astype(jnp.bfloat16).astype(jnp.float32)
+        acts = spread(act_s[...])
+        grads = mg_s[...]
+        for b in (-1, 0, 1):
+            seen = acts[b + 1]
+            sums = (
+                jnp.sum(seen[:-width] * grads[width:], axis=0, keepdims=True),
+                jnp.sum(seen * grads, axis=0, keepdims=True),
+                jnp.sum(seen[width:] * grads[:-width], axis=0, keepdims=True),
+            )
+            for a in (-1, 0, 1):
+                row = 3 * (a + 1) + (b + 1)
+                kern[row : row + 1, hidden] = sums[a + 1] * loss_scale
+        backs = spread(mg_s[...])
+        gathered = stack_rows(
+            *[sum(tap(c, a, b) * backs[1 - b] for b in (-1, 0, 1)) for a in (1, 0, -1)]
+        )
+        pgrad[:, hidden] = (gathered * slope_s[...]).astype(jnp.bfloat16)
+
+    def grad_out(c):
+        left = mixed[:, span(c, block)]
+        for k in range(nnz):
+            gw[1, :, panel(c, k)] = (tn(left, cot[feats(c, k)]) * loss_scale).astype(jnp.bfloat16)
+
+    def grad_in(c):
+        right = pgrad[:, span(c, block)]
+        for k in range(nnz):
+            gw[0, :, panel(c, k)] = (tn(tok[feats(c, k)], right) * loss_scale).astype(jnp.bfloat16)
+
+    limit = tok.shape[0] ** 2
+
+    def token_grad(g):
+        total = jnp.zeros((count, block), jnp.float32)
+        for c in range(cols):
+            at = cols * nnz
+            for k in range(nnz):
+                apart = ids[k, me * cols + c] - g
+                same = 1 - lax.div(apart * apart + (limit - 1), jnp.int32(limit))
+                at += same * (c * nnz + k - at)
+            total += nt(pgrad[:, span(c, block)], w_in[at])
+        return total.astype(jnp.bfloat16)
+
+    return forward, backward, grad_out, grad_in, token_grad
+
+
+def grads_kernel(
+    depth, width, block, cols, nnz, ids, tok_h, cot_h, in_h, out_h, taps,
+    dx_mine, mine, kern_all,
+    tok, cot, w_in, w_out, kern, mixed, pgrad, pre_s, act_s, slope_s, mg_s, gw, gw_part,
+    dx, dx_near, dx_half, dx_far, dx_sum, dx_last, kern_own, kern_part,
+    dx_send, dx_recv, far_send, far_recv, gw_send, gw_recv, part_send, part_recv,
+    kern_send, kern_recv, load_sem,
 ):
     y, r, z, same_chip, across, diagonal = neighbours()
     group = [same_chip, across, diagonal]
-    order = (across, diagonal, same_chip, r)
     tokens, features = dx_mine.shape
-    rows = in_mine.shape[0]
-    lanes = gw_in.shape[1]
-    weights = ((gw_in, in_mine), (gw_out, out_mine))
+    rows = mine.shape[1]
+    half = block // 2
+    lanes = nnz * block
+    per_part = features // block
+    def stack(i, src, dst, at):
+        return pltpu.make_async_copy(src.at[:, span(at, block)], dst.at[at], load_sem.at[i, at])
+
+    def each(i, act):
+        src, dst, many = ((tok_h, tok, tok.shape[0]), (in_h, w_in, cols * nnz), (cot_h, cot, cot.shape[0]))[i]
+
+        def turn(at, carry):
+            act(stack(i, src, dst, at))
+            return carry
+
+        lax.fori_loop(0, many, turn, 0)
+
+    out_load = pltpu.make_async_copy(out_h, w_out, load_sem.at[3, 0])
+    for i in range(3):
+        each(i, lambda copy: copy.start())
+    out_load.start()
+    w_in[cols * nnz] = jnp.zeros((block, block), jnp.bfloat16)
+    kern[...] = jnp.zeros_like(kern)
     enter(
         [{"rows": row} for row in group]
         + [{"crop": 1 - y}]
@@ -342,44 +374,134 @@
         copy.start()
         started.append(copy)
 
-    go(kern, kern_part.at[1, 0], kern_send.at[0], kern_recv.at[1, 0], {"crop": 1 - y})
-    for slot, row in enumerate((diagonal, same_chip)):
-        go(dx.at[span(row, tokens), :], dx_near.at[slot], dx_send.at[slot], dx_recv.at[slot], {"rows": same_chip})
-    for slot, row in enumerate(order):
-        for a in range(2):
-            go(
-                weights[a][0].at[span((1 - y) * 4 + row, rows), :],
-                gw_part.at[a, slot],
-                gw_send.at[a, slot],
-                gw_recv.at[a, slot],
-                {"crop": 1 - y},
-            )
-    dx_loads = [
-        pltpu.make_async_copy(dx.at[span(row, tokens), :], dx_own.at[slot], dx_load.at[slot])
-        for slot, row in enumerate((across, r))
-    ]
-    gw_loads = [
-        [
-            pltpu.make_async_copy(
-                weights[a][0].at[span(y * 4 + row, rows), :], gw_own.at[a, slot], gw_load.at[a, slot]
-            )
-            for a in range(2)
-        ]
-        for slot, row in enumerate(order)
-    ]
-    for load in dx_loads + [load for pair in gw_loads for load in pair]:
-        load.start()
     def arrived(ref, send_sem, recv_sem, target):
         remote(ref, ref, send_sem, recv_sem, target).wait_recv()
 
-    arrived(dx_near.at[0], dx_send.at[0], dx_recv.at[0], {"rows": same_chip})
-    dx_loads[0].wait()
-    dx_half[...] = (
-        dx_own[0].astype(jnp.float32) + dx_near[0].astype(jnp.float32)
-    ).astype(jnp.bfloat16)
+    forward, backward, grad_out, grad_in, token_grad = column_math(
+        width, block, cols, nnz, ids, tok, cot, w_in, w_out, taps, kern, mixed, pgrad,
+        pre_s, act_s, slope_s, mg_s, gw,
+    )
+
+    def give(a, c):
+        go(
+            gw.at[a, span(1 - y, half), span(c, lanes)],
+            gw_part.at[a, c],
+            gw_send.at[a, c],
+            gw_recv.at[a, c],
+            {"crop": 1 - y},
+        )
+
+    def settle(a, c):
+        arrived(gw_part.at[a, c], gw_send.at[a, c], gw_recv.at[a, c], {"crop": 1 - y})
+        gw_part[a, c] = (
+            gw[a, span(y, half), span(c, lanes)].astype(jnp.float32) + gw_part[a, c].astype(jnp.float32)
+        ).astype(jnp.bfloat16)
+        at = span(r * cols + c, lanes)
+        for slot, row in enumerate((across, diagonal, same_chip)):
+            go(
+                gw_part.at[a, c, span(row, rows), :],
+                mine.at[a, :, at],
+                part_send.at[a, c, slot],
+                part_recv.at[a, c, slot],
+                {"rows": row},
+            )
+        mine[a, :, at] = gw_part[a, c, span(r, rows), :]
+
+    def part_of(i):
+        return (z + 1 + i) % depth
+
+    def lanes_of(i):
+        return span(part_of(i), features)
+
+    each(0, lambda copy: copy.wait())
+    each(1, lambda copy: copy.wait())
+    forward(0, lambda: each(2, lambda copy: copy.wait()))
+    grad_out(0)
+    give(1, 0)
+    out_load.wait()
+    backward(0)
+    grad_in(0)
+    give(0, 0)
+
+    def one_column(c, carry):
+        forward(c)
+        backward(c)
+        return carry
+
+    lax.fori_loop(1, cols, one_column, 0)
+
+    near = ((0, diagonal), (1, same_chip))
+
+    def near_copy(slot, row, i):
+        at = lanes_of(i)
+        return remote(
+            dx.at[span(row, tokens), at],
+            dx_near.at[slot, :, at],
+            dx_send.at[slot, i],
+            dx_recv.at[slot, i],
+            {"rows": same_chip},
+        )
+
+    for i in range(depth):
+
+        def one_block(j, carry):
+            g = part_of(i) * per_part + j
+            dx[:, span(g, block)] = token_grad(g)
+            return carry
+
+        lax.fori_loop(0, per_part, one_block, 0)
+        for slot, row in near:
+            near_copy(slot, row, i).start()
+    grad_out(1)
+    give(1, 1)
+    settle(1, 0)
+    for i in range(depth):
+        near_copy(0, diagonal, i).wait_recv()
+        at = lanes_of(i)
+        dx_half[:, at] = (
+            dx[span(across, tokens), at].astype(jnp.float32) + dx_near[0, :, at].astype(jnp.float32)
+        ).astype(jnp.bfloat16)
+        go(dx_half.at[:, at], dx_far.at[:, at], far_send.at[0, i], far_recv.at[0, i], {"rows": across})
+    grad_in(1)
+    give(0, 1)
+    settle(0, 0)
+
+    def later(c, carry):
+        grad_out(c)
+        grad_in(c)
+        return carry
+
+    lax.fori_loop(2, cols, later, 0)
+    for c in range(2, cols):
+        give(1, c)
+        give(0, c)
+    kern_own[...] = kern[...].astype(jnp.bfloat16)
+    go(kern_own, kern_part.at[1, 0], kern_send.at[0], kern_recv.at[1, 0], {"crop": 1 - y})
+
+    def pass_sum(i):
+        at = lanes_of(i)
+        near_copy(1, same_chip, i).wait_recv()
+        arrived(dx_far.at[:, at], far_send.at[0, i], far_recv.at[0, i], {"rows": across})
+        dx_sum[i] = (
+            dx[span(r, tokens), at].astype(jnp.float32)
+            + dx_near[1, :, at].astype(jnp.float32)
+            + dx_far[:, at].astype(jnp.float32)
+        ).astype(jnp.bfloat16)
+        if i < depth - 1:
+            go(
+                dx_sum.at[i],
+                dx_last.at[i],
+                far_send.at[1, i],
+                far_recv.at[1, i],
+                {"hid": part_of(i)},
+            )
+
+    waits = [(a, c) for c in range(1, cols) for a in (1, 0)]
+    sums = list(range(depth))
+    pass_sum(sums.pop(0))
     arrived(kern_part.at[1, 0], kern_send.at[0], kern_recv.at[1, 0], {"crop": 1 - y})
     kern_part[0, r] = (
-        kern[...].astype(jnp.float32) + kern_part[1, 0].astype(jnp.float32)
+        kern_own[...].astype(jnp.float32) + kern_part[1, 0].astype(jnp.float32)
     ).astype(jnp.bfloat16)
     for slot, row in enumerate(group):
         go(
@@ -389,73 +511,47 @@
             kern_recv.at[0, r],
             {"rows": row},
         )
-    go(dx_half, dx_far, dx_send.at[2], dx_recv.at[2], {"rows": across})
-    arrived(dx_near.at[1], dx_send.at[1], dx_recv.at[1], {"rows": same_chip})
-    arrived(dx_far, dx_send.at[2], dx_recv.at[2], {"rows": across})
-    dx_loads[1].wait()
-    for col in range(depth):
-        part = slice(col * features, (col + 1) * features)
-        dx_sum[col] = (
-            dx_own[1, :, part].astype(jnp.float32)
-            + dx_near[1, :, part].astype(jnp.float32)
-            + dx_far[:, part].astype(jnp.float32)
-        ).astype(jnp.bfloat16)
-    for step in range(1, depth):
-        go(
-            dx_sum.at[(z + step) % depth],
-            dx_last.at[step - 1],
-            dx_send.at[2 + step],
-            dx_recv.at[2 + step],
-            {"hid": (z + step) % depth},
-        )
-    for slot, row in enumerate(order):
-        for a in range(2):
-            arrived(gw_part.at[a, slot], gw_send.at[a, slot], gw_recv.at[a, slot], {"crop": 1 - y})
-            gw_loads[slot][a].wait()
-            total = (
-                gw_own[a, slot].astype(jnp.float32)
-                + gw_part[a, slot].astype(jnp.float32)
-            ).astype(jnp.bfloat16)
-            if slot == 3:
-                weights[a][1][:, span(r, lanes)] = total
-            else:
-                gw_sum[a, slot] = total
-                go(
-                    gw_sum.at[a, slot],
-                    weights[a][1].at[:, span(r, lanes)],
-                    gw_send.at[a, 4 + slot],
-                    gw_recv.at[a, 4 + slot],
-                    {"rows": row},
-                )
-    total = dx_sum[z].astype(jnp.float32)
-    for step in range(1, depth):
-        arrived(dx_last.at[step - 1], dx_send.at[2 + step], dx_recv.at[2 + step], {"hid": (z + step) % depth})
-        total += dx_last[step - 1].astype(jnp.float32)
+    while len(waits) > 1:
+        settle(*waits.pop(0))
+        if sums:
+            pass_sum(sums.pop(0))
+    while sums:
+        pass_sum(sums.pop(0))
+    total = dx_sum[depth - 1].astype(jnp.float32)
+    for step in range(depth - 1):
+        arrived(dx_last.at[step], far_send.at[1, step], far_recv.at[1, step], {"hid": part_of(step)})
+        total += dx_last[step].astype(jnp.float32)
     dx_mine[...] = total.astype(jnp.bfloat16)
     for row in group:
         arrived(kern_part.at[0, row], kern_send.at[0], kern_recv.at[0, row], {"rows": same_chip})
     wide = kern.shape[1]
     for row in range(4):
         kern_all[:, row * wide : (row + 1) * wide] = kern_part[0, row].astype(jnp.float32)
-    for slot, row in enumerate(order[:3]):
-        for a in range(2):
-            arrived(
-                weights[a][1].at[:, span(row, lanes)],
-                gw_send.at[a, 4 + slot],
-                gw_recv.at[a, 4 + slot],
-                {"rows": row},
-            )
+    for a, c in waits:
+        settle(a, c)
+    for a in (1, 0):
+        for c in range(cols):
+            for slot, row in enumerate((across, diagonal, same_chip)):
+                arrived(
+                    mine.at[a, :, span(row * cols + c, lanes)],
+                    part_send.at[a, c, slot],
+                    part_recv.at[a, c, slot],
+                    {"rows": row},
+                )
+    for i in range(depth):
+        for slot, row in near:
+            near_copy(slot, row, i).wait_send()
     for copy in started:
         copy.wait_send()
 
 
 def finish_kernel(
-    all_cols, nnz, in_mine, out_mine, dx_mine, kern_all, in_grad, out_grad, dx_grad, kern_grad
+    all_cols, nnz, mine, dx_mine, kern_all, in_grad, out_grad, dx_grad, kern_grad
 ):
     block = in_grad.shape[2]
     dx_grad[...] = dx_mine[...]
     kern_grad[...] = kern_all[: kern_grad.shape[0]]
-    for src, dst in ((in_mine, in_grad), (out_mine, out_grad)):
+    for src, dst in ((mine.at[0], in_grad), (mine.at[1], out_grad)):
         for c in range(all_cols):
             for k in range(nnz):
                 at = (c * nnz + k) * block
@@ -499,60 +595,56 @@
         weight_in.transpose(0, 2, 1, 3).reshape(rows, nnz * all_cols, block),
         weight_out.transpose(0, 2, 1, 3).reshape(rows, nnz * all_cols, block),
     )
-    panel_spec = pl.BlockSpec((block, nnz * block), lambda c: (0, c))
-    dx, gw_in, gw_out, kern = pl.pallas_call(
-        functools.partial(local_kernel, width, block, cols, nnz),
-        name="local_math",
-        out_shape=[
-            sds((whole, model), bf16),
-            sds((block, lanes), bf16),
-            sds((block, lanes), bf16),
-            sds((16, hidden), bf16),
-        ],
-        grid=(cols,),
-        in_specs=[SMEM, VMEM, VMEM, panel_spec, panel_spec, VMEM],
-        out_specs=[VMEM, panel_spec, panel_spec, VMEM],
-        scratch_shapes=[pltpu.VMEM((16, hidden), f32), pltpu.VMEM((whole, model), f32)]
-        + [pltpu.VMEM((whole, block), f32)] * 4,
-        compiler_params=params(),
-    )(block_rows.T, tok_all, cot_all, in_all, out_all, mix_kernel)
     out_rows = block // (n_rows * lax.axis_size("crop"))
-    dx_mine, in_mine, out_mine, kern_all = pl.pallas_call(
-        functools.partial(scatter_kernel, depth),
-        name="scatter_sums",
+    panel = nnz * block
+    dx_mine, mine, kern_all = pl.pallas_call(
+        functools.partial(grads_kernel, depth, width, block, cols, nnz),
+        name="grads_and_sums",
         out_shape=[
             sds((count, features), bf16),
-            sds((out_rows, all_cols * nnz * block), bf16),
-            sds((out_rows, all_cols * nnz * block), bf16),
+            sds((2, out_rows, all_cols * panel), bf16),
             sds((16, hidden * n_rows), f32),
         ],
-        in_specs=[ANY] * 3 + [VMEM],
-        out_specs=[VMEM] * 4,
+        in_specs=[SMEM] + [ANY] * 4 + [VMEM],
+        out_specs=[VMEM] * 3,
         scratch_shapes=[
-            pltpu.VMEM((2, count, model), bf16),
-            pltpu.VMEM((2, 4, out_rows, lanes), bf16),
+            pltpu.VMEM((model // block, whole, block), bf16),
+            pltpu.VMEM((model // block, whole, block), bf16),
+            pltpu.VMEM((cols * nnz + 1, block, block), bf16),
+            pltpu.VMEM((block, lanes), bf16),
+            pltpu.VMEM((16, hidden), f32),
+            pltpu.VMEM((whole, hidden), bf16),
+            pltpu.VMEM((whole, hidden), bf16),
+        ]
+        + [pltpu.VMEM((whole, block), f32)] * 4
+        + [
+            pltpu.VMEM((2, block, lanes), bf16),
+            pltpu.VMEM((2, cols, block // 2, panel), bf16),
+            pltpu.VMEM((whole, model), bf16),
             pltpu.VMEM((2, count, model), bf16),
             pltpu.VMEM((count, model), bf16),
             pltpu.VMEM((count, model), bf16),
             pltpu.VMEM((depth, count, features), bf16),
             pltpu.VMEM((depth - 1, count, features), bf16),
-            pltpu.VMEM((2, 4, out_rows, lanes), bf16),
-            pltpu.VMEM((2, 3, out_rows, lanes), bf16),
+            pltpu.VMEM((16, hidden), bf16),
             pltpu.VMEM((2, n_rows, 16, hidden), bf16),
-            dma((2 + depth,)),
-            dma((2 + depth,)),
-            dma((2, 7)),
-            dma((2, 7)),
+            dma((2, depth)),
+            dma((2, depth)),
+            dma((2, depth)),
+            dma((2, depth)),
+            dma((2, cols)),
+            dma((2, cols)),
+            dma((2, cols, 3)),
+            dma((2, cols, 3)),
             dma((4,)),
             dma((2, n_rows)),
-            dma((2,)),
-            dma((2, 4)),
+            dma((4, max(model // block, cols * nnz))),
         ],
         compiler_params=params(collective_id=2, has_side_effects=True),
-    )(dx, gw_in, gw_out, kern)
+    )(block_rows.T, tok_all, cot_all, in_all, out_all, mix_kernel)
     step = 8
     part = pl.BlockSpec((count * step // out_rows, features), lambda i: (i, 0))
-    flat_spec = pl.BlockSpec((step, all_cols * nnz * block), lambda i: (i, 0))
+    flat_spec = pl.BlockSpec((2, step, all_cols * nnz * block), lambda i: (0, i, 0))
     grad_spec = pl.BlockSpec((step, nnz * all_cols, block), lambda i: (i, 0, 0))
     in_grad, out_grad, dx_grad, kern_grad = pl.pallas_call(
         functools.partial(finish_kernel, all_cols, nnz),
@@ -560,10 +652,10 @@
         grid=(out_rows // step,),
         out_shape=[sds((out_rows, nnz * all_cols, block), f32)] * 2
         + [sds((count, features), bf16), sds(mix_kernel.shape, f32)],
-        in_specs=[flat_spec] * 2 + [part, VMEM],
+        in_specs=[flat_spec, part, VMEM],
         out_specs=[grad_spec] * 2 + [part, VMEM],
         compiler_params=params(),
-    )(in_mine, out_mine, dx_mine, kern_all)
+    )(mine, dx_mine, kern_all)
     in_grad, out_grad = [
         grad.reshape(out_rows, nnz, all_cols, block).transpose(0, 2, 1, 3) for grad in (in_grad, out_grad)
     ]

time: 158 us -> 169 us (1.070)
  Pallas kernels: 158 us -> 168 us
    pallas_call x2 -> x1, Pallas kernels: 85.4 us -> 96.2 us  [split_hidden(): pl.pallas_call(functools.partial(grads_kernel, depth, width, block, cols,...]
where the time goes in v1:
time: 169 us
  Pallas kernels  168 us (99%)
    pallas_call x1, Pallas kernels, split_hidden(): pl.pallas_call(functools.partial(grads_kernel, depth, width, block, cols,...  96.2 us
    pallas_call x1, Pallas kernels, split_hidden(): pl.pallas_call(functools.partial(gather_kernel, depth), name='gather_part...  66.2 us
    pallas_call x1, Pallas kernels, split_hidden(): pl.pallas_call(functools.partial(finish_kernel, all_cols, nnz), name='fin...  5.73 us

profile of v1, /device:TPU:0, one launch (start us, length us, event | category | flops | bytes accessed | tf_op | source)
XLA Modules:
  0.0 168.7 jit_solution(10318050175475005977)
XLA Ops:
  0.6 66.2 %gather_parts.1 = (bf16[512,4096]{1,0:T(8,128)(2,1)}, bf16[512,4096]{1,0:T(8,128)(2,1)}, bf16[256,5120]{1,0:T(8,128)(2,1)}, bf16[256,5120]{1,0:T(8,128)(2,1)}) custom-call(bf16[128,1024]{1,0:T(8,128)(2,1)} %bitcast.18, bf16[128,1024]{1,0:T(8,128)(2,1)} %bitcast.19, bf16[64,80,256]{2,1,0:T(8,128)(2,1)} %bitcast.16, bf16[64,80,256]{2,1,0:T(8,128)(2,1)} %bitcast.17), custom_call_target="tpu_custom_call" | custom-call | tf_op jit(solution)/shard_map/gather_parts/pallas_call | solution.py:574
  66.8 96.2 %grads_and_sums.1 = (bf16[128,1024]{1,0:T(8,128)(2,1)}, bf16[2,32,20480]{2,1,0:T(8,128)(2,1)}, f32[16,4096]{1,0:T(8,128)}) custom-call(s32[5,16]{1,0:T(8,128)} %bitcast.20, bf16[512,4096]{1,0:T(8,128)(2,1)} %get-tuple-element.15.tok_h, bf16[512,4096]{1,0:T(8,128)(2,1)} %get-tuple-element.16.cot_h, bf16[256,5120]{1,0:T(8,128)(2,1)} %get-tuple-element.17.in_h, ...), custom_call_target="tpu_custom_call" | custom-call | tf_op jit(solution)/shard_map/grads_and_sums/pallas_call | solution.py:600
  163.0 5.7 %finish_weights.1 = (f32[32,80,256]{2,1,0:T(8,128)}, f32[32,80,256]{2,1,0:T(8,128)}, bf16[128,1024]{1,0:T(8,128)(2,1)}, f32[9,4096]{1,0:T(8,128)}) custom-call(bf16[2,32,20480]{2,1,0:T(8,128)(2,1)} %get-tuple-element.19.mine, bf16[128,1024]{1,0:T(8,128)(2,1)} %get-tuple-element.20.dx_mine, f32[16,4096]{1,0:T(8,128)} %get-tuple-element.21.kern_all), custom_call_target="tpu_custom_call" | custom-call | tf_op jit(solution)/shard_map/finish_weights/pallas_call | solution.py:649

commit v2 on v1

--- a/solution.py
+++ b/solution.py
@@ -425,10 +425,10 @@
 
     def one_column(c, carry):
         forward(c)
+        grad_out(c)
         backward(c)
+        grad_in(c)
         return carry
-
-    lax.fori_loop(1, cols, one_column, 0)
 
     near = ((0, diagonal), (1, same_chip))
 
@@ -442,41 +442,36 @@
             {"rows": same_chip},
         )
 
-    for i in range(depth):
-
-        def one_block(j, carry):
-            g = part_of(i) * per_part + j
-            dx[:, span(g, block)] = token_grad(g)
-            return carry
-
-        lax.fori_loop(0, per_part, one_block, 0)
-        for slot, row in near:
-            near_copy(slot, row, i).start()
-    grad_out(1)
-    give(1, 1)
-    settle(1, 0)
-    for i in range(depth):
+    def pass_half(i):
         near_copy(0, diagonal, i).wait_recv()
         at = lanes_of(i)
         dx_half[:, at] = (
             dx[span(across, tokens), at].astype(jnp.float32) + dx_near[0, :, at].astype(jnp.float32)
         ).astype(jnp.bfloat16)
         go(dx_half.at[:, at], dx_far.at[:, at], far_send.at[0, i], far_recv.at[0, i], {"rows": across})
-    grad_in(1)
-    give(0, 1)
-    settle(0, 0)
-
-    def later(c, carry):
-        grad_out(c)
-        grad_in(c)
-        return carry
-
-    lax.fori_loop(2, cols, later, 0)
-    for c in range(2, cols):
+
+    for c in range(1, cols):
+        lax.fori_loop(c, c + 1, one_column, 0)
+        if c == cols - 1:
+            settle(1, 0)
+            kern_own[...] = kern[...].astype(jnp.bfloat16)
+            go(kern_own, kern_part.at[1, 0], kern_send.at[0], kern_recv.at[1, 0], {"crop": 1 - y})
         give(1, c)
         give(0, c)
-    kern_own[...] = kern[...].astype(jnp.bfloat16)
-    go(kern_own, kern_part.at[1, 0], kern_send.at[0], kern_recv.at[1, 0], {"crop": 1 - y})
+    settle(0, 0)
+    for i in range(depth):
+
+        def one_block(j, carry):
+            g = part_of(i) * per_part + j
+            dx[:, span(g, block)] = token_grad(g)
+            return carry
+
+        lax.fori_loop(0, per_part, one_block, 0)
+        for slot, row in near:
+            near_copy(slot, row, i).start()
+        if i > 0:
+            pass_half(i - 1)
+    pass_half(depth - 1)
 
     def pass_sum(i):
         at = lanes_of(i)
@@ -498,7 +493,12 @@
 
     waits = [(a, c) for c in range(1, cols) for a in (1, 0)]
     sums = list(range(depth))
-    pass_sum(sums.pop(0))
+    while len(waits) > 2:
+        settle(*waits.pop(0))
+        if sums:
+            pass_sum(sums.pop(0))
+    while sums:
+        pass_sum(sums.pop(0))
     arrived(kern_part.at[1, 0], kern_send.at[0], kern_recv.at[1, 0], {"crop": 1 - y})
     kern_part[0, r] = (
         kern_own[...].astype(jnp.float32) + kern_part[1, 0].astype(jnp.float32)
@@ -511,12 +511,7 @@
             kern_recv.at[0, r],
             {"rows": row},
         )
-    while len(waits) > 1:
-        settle(*waits.pop(0))
-        if sums:
-            pass_sum(sums.pop(0))
-    while sums:
-        pass_sum(sums.pop(0))
+    settle(*waits.pop(0))
     total = dx_sum[depth - 1].astype(jnp.float32)
     for step in range(depth - 1):
         arrived(dx_last.at[step], far_send.at[1, step], far_recv.at[1, step], {"hid": part_of(step)})

time: 169 us -> 150 us (0.89)
  Pallas kernels: 168 us -> 149 us
    pallas_call x1, Pallas kernels: 96.2 us -> 77.4 us  [split_hidden(): pl.pallas_call(functools.partial(grads_kernel, depth, width, block, cols,...]
where the time goes in v2:
time: 150 us
  Pallas kernels  149 us (99%)
    pallas_call x1, Pallas kernels, split_hidden(): pl.pallas_call(functools.partial(grads_kernel, depth, width, block, cols,...  77.4 us
    pallas_call x1, Pallas kernels, split_hidden(): pl.pallas_call(functools.partial(gather_kernel, depth), name='gather_part...  66.2 us
    pallas_call x1, Pallas kernels, split_hidden(): pl.pallas_call(functools.partial(finish_kernel, all_cols, nnz), name='fin...  5.73 us

profile of v2, /device:TPU:0, one launch (start us, length us, event | category | flops | bytes accessed | tf_op | source)
XLA Modules:
  0.0 150.0 jit_solution(14755282470500432268)
XLA Ops:
  0.6 66.2 %gather_parts.1 = (bf16[512,4096]{1,0:T(8,128)(2,1)}, bf16[512,4096]{1,0:T(8,128)(2,1)}, bf16[256,5120]{1,0:T(8,128)(2,1)}, bf16[256,5120]{1,0:T(8,128)(2,1)}) custom-call(bf16[128,1024]{1,0:T(8,128)(2,1)} %bitcast.18, bf16[128,1024]{1,0:T(8,128)(2,1)} %bitcast.19, bf16[64,80,256]{2,1,0:T(8,128)(2,1)} %bitcast.16, bf16[64,80,256]{2,1,0:T(8,128)(2,1)} %bitcast.17), custom_call_target="tpu_custom_call" | custom-call | tf_op jit(solution)/shard_map/gather_parts/pallas_call | solution.py:569
  66.8 77.4 %grads_and_sums.1 = (bf16[128,1024]{1,0:T(8,128)(2,1)}, bf16[2,32,20480]{2,1,0:T(8,128)(2,1)}, f32[16,4096]{1,0:T(8,128)}) custom-call(s32[5,16]{1,0:T(8,128)} %bitcast.20, bf16[512,4096]{1,0:T(8,128)(2,1)} %get-tuple-element.15.tok_h, bf16[512,4096]{1,0:T(8,128)(2,1)} %get-tuple-element.16.cot_h, bf16[256,5120]{1,0:T(8,128)(2,1)} %get-tuple-element.17.in_h, ...), custom_call_target="tpu_custom_call" | custom-call | tf_op jit(solution)/shard_map/grads_and_sums/pallas_call | solution.py:595
  144.2 5.7 %finish_weights.1 = (f32[32,80,256]{2,1,0:T(8,128)}, f32[32,80,256]{2,1,0:T(8,128)}, bf16[128,1024]{1,0:T(8,128)(2,1)}, f32[9,4096]{1,0:T(8,128)}) custom-call(bf16[2,32,20480]{2,1,0:T(8,128)(2,1)} %get-tuple-element.19.mine, bf16[128,1024]{1,0:T(8,128)(2,1)} %get-tuple-element.20.dx_mine, f32[16,4096]{1,0:T(8,128)} %get-tuple-element.21.kern_all), custom_call_target="tpu_custom_call" | custom-call | tf_op jit(solution)/shard_map/finish_weights/pallas_call | solution.py:644

commit v3 on v2

--- a/solution.py
+++ b/solution.py
@@ -48,29 +48,38 @@
     )
 
 
-def gather_kernel(
-    depth, tok, cot, w_in, w_out, tok_all, cot_all, in_all, out_all,
+def gather_stage(
+    depth, partners, tok_h, cot_h, in_h, out_h, tok, cot, w_in, w_out,
     raw, flat, stage, tok_send, tok_recv, w_send, w_recv, own_sem, raw_sem,
 ):
     y, r, z, same_chip, across, diagonal = neighbours()
-    tokens, features = tok.shape
-    rows = w_in.shape[0]
-    lanes = in_all.shape[1]
+    tokens, features = tok_h.shape
+    rows = in_h.shape[0]
     half = rows // 2
-    block = w_in.shape[2]
+    block = tok.shape[2]
+    per_part = features // block
+    panels_own = w_out.shape[0]
     all_cols = stage.shape[1] // rows
-    nnz = w_in.shape[1] // all_cols
+    nnz = in_h.shape[1] // all_cols
+    own = [
+        pltpu.make_async_copy(
+            src.at[:, j * block : (j + 1) * block],
+            full.at[z * per_part + j, span(r, tokens), :],
+            own_sem.at[a, j],
+        )
+        for a, (src, full) in enumerate(((tok_h, tok), (cot_h, cot)))
+        for j in range(per_part)
+    ]
     loads = [
-        pltpu.make_async_copy(src, raw.at[a], raw_sem.at[a]) for a, src in enumerate((w_in, w_out))
+        pltpu.make_async_copy(src, raw.at[a], raw_sem.at[a]) for a, src in enumerate((in_h, out_h))
     ]
-    for load in loads:
+    for load in own + loads:
         load.start()
-    enter(
-        [{"rows": same_chip}, {"rows": across}, {"rows": diagonal}, {"crop": 1 - y}]
-        + [{"hid": (z + step) % depth} for step in range(1, depth)]
-    )
-    streams = ((tok, tok_all), (cot, cot_all))
-    panels = ((flat.at[0], in_all), (flat.at[1], out_all))
+    enter(partners)
+    for load in own:
+        load.wait()
+    streams = (tok, cot)
+    panels = ((flat.at[0], w_in), (flat.at[1], w_out))
     targets = ({"hid": z + 1}, {"hid": z - 1}, {"rows": across}, {"rows": same_chip})
     has_up, has_down = z + 1 < depth, z >= 1
     sends, local = [], []
@@ -83,14 +92,14 @@
             pl.when(have)(lambda: make().start())
 
     def piece(full, row, col):
-        return full.at[span(row, tokens), span(col, features)]
-
-    def pass_on(a, which, col, kind, have=None, own=False):
+        return full.at[span(col, per_part), span(row, tokens), :]
+
+    def pass_on(a, which, col, kind, have=None):
         def make():
             row = (r, across)[which]
-            part = piece(streams[a][1], row, col)
+            part = piece(streams[a], row, col)
             return remote(
-                streams[a][0] if own else part,
+                part,
                 part,
                 tok_send.at[a, which, col, kind],
                 tok_recv.at[a, row, col],
@@ -101,7 +110,7 @@
 
     def await_piece(a, row, col, have=None):
         def wait():
-            part = piece(streams[a][1], row, col)
+            part = piece(streams[a], row, col)
             remote(
                 part, part, tok_send.at[a, 0, 0, 3], tok_recv.at[a, row, col], {"rows": same_chip}
             ).wait_recv()
@@ -112,7 +121,11 @@
             pl.when(have)(wait)
 
     def half_rows(full, row, h):
-        return full.at[pl.ds(pl.multiple_of(row * rows + h * half, half), half), :]
+        at = pl.ds(pl.multiple_of(row * rows + h * half, half), half)
+        return full.at[pl.ds(0, panels_own), at, :]
+
+    def whole_rows(full, row):
+        return full.at[pl.ds(0, panels_own), span(row, rows), :]
 
     def flatten(a):
         def turn(k, carry):
@@ -121,7 +134,7 @@
                 stage[h] = part.astype(jnp.float32).reshape(rows * all_cols, 128)
             for c in range(all_cols):
                 for h in range(block // 128):
-                    flat[a, :, pl.ds(pl.multiple_of((c * nnz + k) * block + h * 128, 128), 128)] = stage[
+                    flat[a, c * nnz + k, :, h * 128 : (h + 1) * 128] = stage[
                         h, pl.ds(c, rows, stride=all_cols), :
                     ].astype(jnp.bfloat16)
             return carry
@@ -135,7 +148,7 @@
         for slot, dest in ((1, across), (2, diagonal)):
             launch(
                 lambda slot=slot, dest=dest: remote(
-                    src.at[span(y, half), span(dest, lanes)],
+                    src.at[span(dest, panels_own), span(y, half), :],
                     half_rows(full, r, y),
                     w_send.at[a, slot],
                     w_recv.at[a, r, y],
@@ -144,15 +157,15 @@
             )
         launch(
             lambda: remote(
-                src.at[:, span(same_chip, lanes)],
-                full.at[span(r, rows), :],
+                src.at[span(same_chip, panels_own)],
+                whole_rows(full, r),
                 w_send.at[a, 0],
                 w_recv.at[a, r, 0],
                 {"rows": same_chip},
             )
         )
         keep = pltpu.make_async_copy(
-            src.at[:, span(r, lanes)], full.at[span(r, rows), :], own_sem.at[a, 1]
+            src.at[span(r, panels_own)], whole_rows(full, r), own_sem.at[a, per_part]
         )
         keep.start()
         local.append(keep)
@@ -181,11 +194,7 @@
                 pass_on(a, which, col, 3, have)
 
     for a, kind in ((1, 2), (0, 0), (0, 1), (1, 0), (1, 1), (0, 2), (0, 3), (1, 3)):
-        pass_on(a, 0, z, kind, (has_up, has_down, None, None)[kind], own=True)
-    for a in range(2):
-        keep = pltpu.make_async_copy(streams[a][0], piece(streams[a][1], r, z), own_sem.at[a, 0])
-        keep.start()
-        local.append(keep)
+        pass_on(a, 0, z, kind, (has_up, has_down, None, None)[kind])
     give_weights(0)
     await_piece(1, across, z)
     for kind in (0, 1, 3):
@@ -203,7 +212,7 @@
         pass_on(0, 1, col, 3)
     for a in range(2):
         full = panels[a][1]
-        part = full.at[span(same_chip, rows), :]
+        part = whole_rows(full, same_chip)
         remote(
             part, part, w_send.at[a, 0], w_recv.at[a, same_chip, 0], {"rows": same_chip}
         ).wait_recv()
@@ -217,11 +226,15 @@
                 await_piece(a, row, (z + step) % depth)
     for copy in local:
         copy.wait()
-    for make, have in sends:
-        if have is None:
-            make().wait_send()
-        else:
-            pl.when(have)(lambda make=make: make().wait_send())
+
+    def drain():
+        for make, have in sends:
+            if have is None:
+                make().wait_send()
+            else:
+                pl.when(have)(lambda make=make: make().wait_send())
+
+    return drain
 
 
 def nt(a, b):
@@ -260,7 +273,7 @@
         row = 3 * (a + 1) + (b + 1)
         return taps[row : row + 1, span(me * cols + c, block)]
 
-    def forward(c, ready=None):
+    def forward(c):
         hidden = span(c, block)
         pre = jnp.dot(tok[feats(c, 0)], w_in[c * nnz], preferred_element_type=jnp.float32)
         for k in range(1, nnz):
@@ -276,14 +289,12 @@
         mixed[:, hidden] = stack_rows(
             *[sum(tap(c, a, b) * acts[b + 1] for b in (-1, 0, 1)) for a in (-1, 0, 1)]
         ).astype(jnp.bfloat16)
-        if ready is not None:
-            ready()
 
     def backward(c):
         hidden = span(c, block)
-        mg = nt(cot[feats(c, 0)], w_out[:, panel(c, 0)])
+        mg = nt(cot[feats(c, 0)], w_out[c * nnz])
         for k in range(1, nnz):
-            mg += nt(cot[feats(c, k)], w_out[:, panel(c, k)])
+            mg += nt(cot[feats(c, k)], w_out[c * nnz + k])
         mg_s[...] = mg.astype(jnp.bfloat16).astype(jnp.float32)
         acts = spread(act_s[...])
         grads = mg_s[...]
@@ -332,10 +343,10 @@
 def grads_kernel(
     depth, width, block, cols, nnz, ids, tok_h, cot_h, in_h, out_h, taps,
     dx_mine, mine, kern_all,
-    tok, cot, w_in, w_out, kern, mixed, pgrad, pre_s, act_s, slope_s, mg_s, gw, gw_part,
+    tok, cot, w_in, w_out, raw, flat, stage, tok_send, tok_recv, w_send, w_recv, own_sem, raw_sem, kern, mixed, pgrad, pre_s, act_s, slope_s, mg_s, gw, gw_part,
     dx, dx_near, dx_half, dx_far, dx_sum, dx_last, kern_own, kern_part,
     dx_send, dx_recv, far_send, far_recv, gw_send, gw_recv, part_send, part_recv,
-    kern_send, kern_recv, load_sem,
+    kern_send, kern_recv,
 ):
     y, r, z, same_chip, across, diagonal = neighbours()
     group = [same_chip, across, diagonal]
@@ -344,28 +355,15 @@
     half = block // 2
     lanes = nnz * block
     per_part = features // block
-    def stack(i, src, dst, at):
-        return pltpu.make_async_copy(src.at[:, span(at, block)], dst.at[at], load_sem.at[i, at])
-
-    def each(i, act):
-        src, dst, many = ((tok_h, tok, tok.shape[0]), (in_h, w_in, cols * nnz), (cot_h, cot, cot.shape[0]))[i]
-
-        def turn(at, carry):
-            act(stack(i, src, dst, at))
-            return carry
-
-        lax.fori_loop(0, many, turn, 0)
-
-    out_load = pltpu.make_async_copy(out_h, w_out, load_sem.at[3, 0])
-    for i in range(3):
-        each(i, lambda copy: copy.start())
-    out_load.start()
     w_in[cols * nnz] = jnp.zeros((block, block), jnp.bfloat16)
     kern[...] = jnp.zeros_like(kern)
-    enter(
+    drain = gather_stage(
+        depth,
         [{"rows": row} for row in group]
         + [{"crop": 1 - y}]
-        + [{"hid": (z + step) % depth} for step in range(1, depth)]
+        + [{"hid": (z + step) % depth} for step in range(1, depth)],
+        tok_h, cot_h, in_h, out_h, tok, cot, w_in, w_out,
+        raw, flat, stage, tok_send, tok_recv, w_send, w_recv, own_sem, raw_sem,
     )
     started = []
 
@@ -382,14 +380,17 @@
         pre_s, act_s, slope_s, mg_s, gw,
     )
 
-    def give(a, c):
-        go(
+    def give_copy(a, c):
+        return remote(
             gw.at[a, span(1 - y, half), span(c, lanes)],
             gw_part.at[a, c],
             gw_send.at[a, c],
             gw_recv.at[a, c],
             {"crop": 1 - y},
         )
+
+    def give(a, c):
+        give_copy(a, c).start()
 
     def settle(a, c):
         arrived(gw_part.at[a, c], gw_send.at[a, c], gw_recv.at[a, c], {"crop": 1 - y})
@@ -413,12 +414,9 @@
     def lanes_of(i):
         return span(part_of(i), features)
 
-    each(0, lambda copy: copy.wait())
-    each(1, lambda copy: copy.wait())
-    forward(0, lambda: each(2, lambda copy: copy.wait()))
+    forward(0)
     grad_out(0)
     give(1, 0)
-    out_load.wait()
     backward(0)
     grad_in(0)
     give(0, 0)
@@ -450,7 +448,14 @@
         ).astype(jnp.bfloat16)
         go(dx_half.at[:, at], dx_far.at[:, at], far_send.at[0, i], far_recv.at[0, i], {"rows": across})
 
-    for c in range(1, cols):
+    def inner_column(c, carry):
+        one_column(c, carry)
+        for a in (1, 0):
+            give_copy(a, c).start()
+        return carry
+
+    lax.fori_loop(1, cols - 1, inner_column, 0)
+    for c in range(cols - 1, cols):
         lax.fori_loop(c, c + 1, one_column, 0)
         if c == cols - 1:
             settle(1, 0)
@@ -538,19 +543,28 @@
             near_copy(slot, row, i).wait_send()
     for copy in started:
         copy.wait_send()
+    for a in range(2):
+        for c in range(cols):
+            give_copy(a, c).wait_send()
+    drain()
 
 
 def finish_kernel(
-    all_cols, nnz, mine, dx_mine, kern_all, in_grad, out_grad, dx_grad, kern_grad
+    all_cols, nnz, mine, dx_mine, kern_all, in_grad, out_grad, dx_grad, kern_grad, stage
 ):
-    block = in_grad.shape[2]
+    block = in_grad.shape[1]
+    step = mine.shape[1]
     dx_grad[...] = dx_mine[...]
     kern_grad[...] = kern_all[: kern_grad.shape[0]]
     for src, dst in ((mine.at[0], in_grad), (mine.at[1], out_grad)):
-        for c in range(all_cols):
-            for k in range(nnz):
-                at = (c * nnz + k) * block
-                dst[:, k * all_cols + c, :] = src[:, at : at + block].astype(jnp.float32)
+        for h in range(block // 128):
+            for c in range(all_cols):
+                for k in range(nnz):
+                    at = (c * nnz + k) * block + h * 128
+                    stage[h, pl.ds(k * all_cols + c, step, stride=nnz * all_cols), :] = src[
+                        :, at : at + 128
+                    ].astype(jnp.float32)
+            dst[:, h * 128 : (h + 1) * 128] = stage[h]
 
 
 def split_hidden(tokens, cotangent, weight_in, weight_out, mix_kernel, block_rows):
@@ -566,30 +580,6 @@
     bf16, f32 = jnp.bfloat16, jnp.float32
     dma, sds = pltpu.SemaphoreType.DMA, jax.ShapeDtypeStruct
     params = functools.partial(pltpu.CompilerParams, vmem_limit_bytes=60 * 1024 * 1024)
-    tok_all, cot_all, in_all, out_all = pl.pallas_call(
-        functools.partial(gather_kernel, depth),
-        name="gather_parts",
-        out_shape=[sds((whole, model), bf16)] * 2 + [sds((rows * n_rows, lanes), bf16)] * 2,
-        in_specs=[ANY] * 4,
-        out_specs=[ANY] * 4,
-        scratch_shapes=[
-            pltpu.VMEM((2, rows, nnz * all_cols, block), bf16),
-            pltpu.VMEM((2, rows, all_cols * nnz * block), bf16),
-            pltpu.VMEM((block // 128, rows * all_cols, 128), f32),
-            dma((2, 2, depth, 4)),
-            dma((2, n_rows, depth)),
-            dma((2, 5)),
-            dma((2, n_rows, 2)),
-            dma((2, 2)),
-            dma((2,)),
-        ],
-        compiler_params=params(collective_id=1, has_side_effects=True),
-    )(
-        tokens.reshape(count, features),
-        cotangent.reshape(count, features),
-        weight_in.transpose(0, 2, 1, 3).reshape(rows, nnz * all_cols, block),
-        weight_out.transpose(0, 2, 1, 3).reshape(rows, nnz * all_cols, block),
-    )
     out_rows = block // (n_rows * lax.axis_size("crop"))
     panel = nnz * block
     dx_mine, mine, kern_all = pl.pallas_call(
@@ -606,7 +596,16 @@
             pltpu.VMEM((model // block, whole, block), bf16),
             pltpu.VMEM((model // block, whole, block), bf16),
             pltpu.VMEM((cols * nnz + 1, block, block), bf16),
-            pltpu.VMEM((block, lanes), bf16),
+            pltpu.VMEM((cols * nnz, block, block), bf16),
+            pltpu.VMEM((2, rows, nnz * all_cols, block), bf16),
+            pltpu.VMEM((2, all_cols * nnz, rows, block), bf16),
+            pltpu.VMEM((block // 128, rows * all_cols, 128), f32),
+            dma((2, 2, depth, 4)),
+            dma((2, n_rows, depth)),
+            dma((2, 5)),
+            dma((2, n_rows, 2)),
+            dma((2, features // block + 1)),
+            dma((2,)),
             pltpu.VMEM((16, hidden), f32),
             pltpu.VMEM((whole, hidden), bf16),
             pltpu.VMEM((whole, hidden), bf16),
@@ -633,22 +632,29 @@
             dma((2, cols, 3)),
             dma((4,)),
             dma((2, n_rows)),
-            dma((4, max(model // block, cols * nnz))),
         ],
         compiler_params=params(collective_id=2, has_side_effects=True),
-    )(block_rows.T, tok_all, cot_all, in_all, out_all, mix_kernel)
+    )(
+        block_rows.T,
+        tokens.reshape(count, features),
+        cotangent.reshape(count, features),
+        weight_in.transpose(0, 2, 1, 3).reshape(rows, nnz * all_cols, block),
+        weight_out.transpose(0, 2, 1, 3).reshape(rows, nnz * all_cols, block),
+        mix_kernel,
+    )
     step = 8
     part = pl.BlockSpec((count * step // out_rows, features), lambda i: (i, 0))
     flat_spec = pl.BlockSpec((2, step, all_cols * nnz * block), lambda i: (0, i, 0))
-    grad_spec = pl.BlockSpec((step, nnz * all_cols, block), lambda i: (i, 0, 0))
+    grad_spec = pl.BlockSpec((step * nnz * all_cols, block), lambda i: (i, 0))
     in_grad, out_grad, dx_grad, kern_grad = pl.pallas_call(
         functools.partial(finish_kernel, all_cols, nnz),
         name="finish_weights",
         grid=(out_rows // step,),
-        out_shape=[sds((out_rows, nnz * all_cols, block), f32)] * 2
+        out_shape=[sds((out_rows * nnz * all_cols, block), f32)] * 2
         + [sds((count, features), bf16), sds(mix_kernel.shape, f32)],
         in_specs=[flat_spec, part, VMEM],
         out_specs=[grad_spec] * 2 + [part, VMEM],
+        scratch_shapes=[pltpu.VMEM((block // 128, step * nnz * all_cols, 128), f32)],
         compiler_params=params(),
     )(mine, dx_mine, kern_all)
     in_grad, out_grad = [

time: 150 us -> 145 us (0.967)
  Pallas kernels: 149 us -> 144 us
    pallas_call x1 -> x0, Pallas kernels: 66.2 us -> none  [split_hidden(): pl.pallas_call(functools.partial(gather_kernel, depth), name='gather_part...]
    pallas_call x1, Pallas kernels: 77.4 us -> 139 us  [split_hidden(): pl.pallas_call(functools.partial(grads_kernel, depth, width, block, cols,...]
where the time goes in v3:
time: 145 us
  Pallas kernels  144 us (99%)
    pallas_call x1, Pallas kernels, split_hidden(): pl.pallas_call(functools.partial(grads_kernel, depth, width, block, cols,...  139 us
    pallas_call x1, Pallas kernels, split_hidden(): pl.pallas_call(functools.partial(finish_kernel, all_cols, nnz), name='fin...  5.73 us

profile of v3, /device:TPU:0, one launch (start us, length us, event | category | flops | bytes accessed | tf_op | source)
XLA Modules:
  0.0 145.2 jit_solution(14509710672287857417)
XLA Ops:
  0.6 138.7 %grads_and_sums.1 = (bf16[128,1024]{1,0:T(8,128)(2,1)}, bf16[2,32,20480]{2,1,0:T(8,128)(2,1)}, f32[16,4096]{1,0:T(8,128)}) custom-call(s32[5,16]{1,0:T(8,128)} %bitcast.20, bf16[128,1024]{1,0:T(8,128)(2,1)} %bitcast.18, bf16[128,1024]{1,0:T(8,128)(2,1)} %bitcast.19, bf16[64,80,256]{2,1,0:T(8,128)(2,1)} %bitcast.16, bf16[64,80,256]{2,1,0:T(8,128)(2,1)} %bitcast.17, ...), custom_call_target="tpu_custom_call" | custom-call | tf_op jit(solution)/shard_map/grads_and_sums/pallas_call | solution.py:585
  139.4 5.7 %finish_weights.1 = (f32[2560,256]{1,0:T(8,128)}, f32[2560,256]{1,0:T(8,128)}, bf16[128,1024]{1,0:T(8,128)(2,1)}, f32[9,4096]{1,0:T(8,128)}) custom-call(bf16[2,32,20480]{2,1,0:T(8,128)(2,1)} %get-tuple-element.11.mine, bf16[128,1024]{1,0:T(8,128)(2,1)} %get-tuple-element.12.dx_mine, f32[16,4096]{1,0:T(8,128)} %get-tuple-element.13.kern_all), custom_call_target="tpu_custom_call" | custom-call | tf_op jit(solution)/shard_map/finish_weights/pallas_call | solution.py:649

commit v4 on v3

--- a/solution.py
+++ b/solution.py
@@ -67,7 +67,7 @@
             full.at[z * per_part + j, span(r, tokens), :],
             own_sem.at[a, j],
         )
-        for a, (src, full) in enumerate(((tok_h, tok), (cot_h, cot)))
+        for a, (src, full) in enumerate(((cot_h, cot), (tok_h, tok)))
         for j in range(per_part)
     ]
     loads = [
@@ -78,7 +78,7 @@
     enter(partners)
     for load in own:
         load.wait()
-    streams = (tok, cot)
+    streams = (cot, tok)
     panels = ((flat.at[0], w_in), (flat.at[1], w_out))
     targets = ({"hid": z + 1}, {"hid": z - 1}, {"rows": across}, {"rows": same_chip})
     has_up, has_down = z + 1 < depth, z >= 1
@@ -206,11 +206,12 @@
             mirror_weights(step - 1)
     for a in range(depth - 1, 2):
         mirror_weights(a)
-    for step in range(depth):
-        col = (z + step) % depth
-        await_piece(0, across, col)
-        pass_on(0, 1, col, 3)
-    for a in range(2):
+    def await_rows(a):
+        for row in (same_chip, diagonal):
+            for step in range(depth):
+                await_piece(a, row, (z + step) % depth)
+
+    def await_weights(a):
         full = panels[a][1]
         part = whole_rows(full, same_chip)
         remote(
@@ -221,11 +222,18 @@
             remote(
                 part, part, w_send.at[a, 0], w_recv.at[a, row, 1 - y], {"crop": 1 - y}
             ).wait_recv()
-        for row in (same_chip, diagonal):
-            for step in range(depth):
-                await_piece(a, row, (z + step) % depth)
-    for copy in local:
-        copy.wait()
+        local[a].wait()
+
+    await_rows(1)
+    await_weights(0)
+
+    def await_rest():
+        for step in range(depth):
+            col = (z + step) % depth
+            await_piece(0, across, col)
+            pass_on(0, 1, col, 3)
+        await_weights(1)
+        await_rows(0)
 
     def drain():
         for make, have in sends:
@@ -234,7 +242,7 @@
             else:
                 pl.when(have)(lambda make=make: make().wait_send())
 
-    return drain
+    return await_rest, drain
 
 
 def nt(a, b):
@@ -357,7 +365,7 @@
     per_part = features // block
     w_in[cols * nnz] = jnp.zeros((block, block), jnp.bfloat16)
     kern[...] = jnp.zeros_like(kern)
-    drain = gather_stage(
+    await_rest, drain = gather_stage(
         depth,
         [{"rows": row} for row in group]
         + [{"crop": 1 - y}]
@@ -380,25 +388,30 @@
         pre_s, act_s, slope_s, mg_s, gw,
     )
 
-    def give_copy(a, c):
+    def give_copy(a, c, far):
+        side = (r // 2, 1 - r // 2)[far]
         return remote(
-            gw.at[a, span(1 - y, half), span(c, lanes)],
-            gw_part.at[a, c],
-            gw_send.at[a, c],
-            gw_recv.at[a, c],
+            gw.at[a, span((1 - y) * 2 + side, half // 2), span(c, lanes)],
+            gw_part.at[a, c, span(side, half // 2), :],
+            gw_send.at[a, c, far],
+            gw_recv.at[a, c, far],
             {"crop": 1 - y},
         )
 
     def give(a, c):
-        give_copy(a, c).start()
-
-    def settle(a, c):
-        arrived(gw_part.at[a, c], gw_send.at[a, c], gw_recv.at[a, c], {"crop": 1 - y})
-        gw_part[a, c] = (
-            gw[a, span(y, half), span(c, lanes)].astype(jnp.float32) + gw_part[a, c].astype(jnp.float32)
+        for far in (1, 0):
+            give_copy(a, c, far).start()
+
+    def settle_side(a, c, far):
+        side = (r // 2, 1 - r // 2)[far]
+        at = span(side, half // 2)
+        give_copy(a, c, far).wait_recv()
+        gw_part[a, c, at, :] = (
+            gw[a, span(y * 2 + side, half // 2), span(c, lanes)].astype(jnp.float32)
+            + gw_part[a, c, at, :].astype(jnp.float32)
         ).astype(jnp.bfloat16)
         at = span(r * cols + c, lanes)
-        for slot, row in enumerate((across, diagonal, same_chip)):
+        for slot, row in ((0, across), (1, diagonal)) if far else ((2, same_chip),):
             go(
                 gw_part.at[a, c, span(row, rows), :],
                 mine.at[a, :, at],
@@ -406,7 +419,12 @@
                 part_recv.at[a, c, slot],
                 {"rows": row},
             )
-        mine[a, :, at] = gw_part[a, c, span(r, rows), :]
+        if not far:
+            mine[a, :, at] = gw_part[a, c, span(r, rows), :]
+
+    def settle(a, c):
+        settle_side(a, c, 1)
+        settle_side(a, c, 0)
 
     def part_of(i):
         return (z + 1 + i) % depth
@@ -415,6 +433,7 @@
         return span(part_of(i), features)
 
     forward(0)
+    await_rest()
     grad_out(0)
     give(1, 0)
     backward(0)
@@ -450,19 +469,22 @@
 
     def inner_column(c, carry):
         one_column(c, carry)
+
+        @pl.when(c == cols - 1)
+        def _():
+            kern_own[...] = kern[...].astype(jnp.bfloat16)
+            kern_copy.start()
+
         for a in (1, 0):
-            give_copy(a, c).start()
+            give(a, c)
         return carry
 
-    lax.fori_loop(1, cols - 1, inner_column, 0)
-    for c in range(cols - 1, cols):
-        lax.fori_loop(c, c + 1, one_column, 0)
-        if c == cols - 1:
-            settle(1, 0)
-            kern_own[...] = kern[...].astype(jnp.bfloat16)
-            go(kern_own, kern_part.at[1, 0], kern_send.at[0], kern_recv.at[1, 0], {"crop": 1 - y})
-        give(1, c)
-        give(0, c)
+    kern_copy = remote(
+        kern_own, kern_part.at[1, 0], kern_send.at[0], kern_recv.at[1, 0], {"crop": 1 - y}
+    )
+    lax.fori_loop(1, 2, inner_column, 0)
+    settle(1, 0)
+    lax.fori_loop(2, cols, inner_column, 0)
     settle(0, 0)
     for i in range(depth):
 
@@ -504,7 +526,7 @@
             pass_sum(sums.pop(0))
     while sums:
         pass_sum(sums.pop(0))
-    arrived(kern_part.at[1, 0], kern_send.at[0], kern_recv.at[1, 0], {"crop": 1 - y})
+    kern_copy.wait_recv()
     kern_part[0, r] = (
         kern_own[...].astype(jnp.float32) + kern_part[1, 0].astype(jnp.float32)
     ).astype(jnp.bfloat16)
@@ -543,9 +565,11 @@
             near_copy(slot, row, i).wait_send()
     for copy in started:
         copy.wait_send()
+    kern_copy.wait_send()
     for a in range(2):
         for c in range(cols):
-            give_copy(a, c).wait_send()
+            for far in range(2):
+                give_copy(a, c, far).wait_send()
     drain()
 
 
@@ -626,8 +650,8 @@
             dma((2, depth)),
             dma((2, depth)),
             dma((2, depth)),
-            dma((2, cols)),
-            dma((2, cols)),
+            dma((2, cols, 2)),
+            dma((2, cols, 2)),
             dma((2, cols, 3)),
             dma((2, cols, 3)),
             dma((4,)),
@@ -787,6 +811,7 @@
             and n_rows == 4
             and tokens.shape[0] == 1
             and weight_in.shape[1] % n_rows == 0
+            and weight_in.shape[1] >= 2 * n_rows
             and tokens.shape[1] * tokens.shape[2] * n_rows * tokens.shape[3] * n_hid <= 2**22
         )
         chosen = split_hidden if fits else on_device

time: 145 us -> 144 us (level)
    pallas_call x1, Pallas kernels: 139 us -> 137 us  [split_hidden(): pl.pallas_call(functools.partial(grads_kernel, depth, width, block, cols,...]
where the time goes in v4:
time: 144 us
  Pallas kernels  143 us (99%)
    pallas_call x1, Pallas kernels, split_hidden(): pl.pallas_call(functools.partial(grads_kernel, depth, width, block, cols,...  137 us
    pallas_call x1, Pallas kernels, split_hidden(): pl.pallas_call(functools.partial(finish_kernel, all_cols, nnz), name='fin...  5.73 us

profile of v4, /device:TPU:0, one launch (start us, length us, event | category | flops | bytes accessed | tf_op | source)
XLA Modules:
  0.0 143.8 jit_solution(7250201484371528252)
XLA Ops:
  0.6 137.3 %grads_and_sums.1 = (bf16[128,1024]{1,0:T(8,128)(2,1)}, bf16[2,32,20480]{2,1,0:T(8,128)(2,1)}, f32[16,4096]{1,0:T(8,128)}) custom-call(s32[5,16]{1,0:T(8,128)} %bitcast.20, bf16[128,1024]{1,0:T(8,128)(2,1)} %bitcast.18, bf16[128,1024]{1,0:T(8,128)(2,1)} %bitcast.19, bf16[64,80,256]{2,1,0:T(8,128)(2,1)} %bitcast.16, bf16[64,80,256]{2,1,0:T(8,128)(2,1)} %bitcast.17, ...), custom_call_target="tpu_custom_call" | custom-call | tf_op jit(solution)/shard_map/grads_and_sums/pallas_call | solution.py:609
  137.9 5.7 %finish_weights.1 = (f32[2560,256]{1,0:T(8,128)}, f32[2560,256]{1,0:T(8,128)}, bf16[128,1024]{1,0:T(8,128)(2,1)}, f32[9,4096]{1,0:T(8,128)}) custom-call(bf16[2,32,20480]{2,1,0:T(8,128)(2,1)} %get-tuple-element.11.mine, bf16[128,1024]{1,0:T(8,128)(2,1)} %get-tuple-element.12.dx_mine, f32[16,4096]{1,0:T(8,128)} %get-tuple-element.13.kern_all), custom_call_target="tpu_custom_call" | custom-call | tf_op jit(solution)/shard_map/finish_weights/pallas_call | solution.py:673

commit v5 on v4

--- a/solution.py
+++ b/solution.py
@@ -352,7 +352,7 @@
     depth, width, block, cols, nnz, ids, tok_h, cot_h, in_h, out_h, taps,
     dx_mine, mine, kern_all,
     tok, cot, w_in, w_out, raw, flat, stage, tok_send, tok_recv, w_send, w_recv, own_sem, raw_sem, kern, mixed, pgrad, pre_s, act_s, slope_s, mg_s, gw, gw_part,
-    dx, dx_near, dx_half, dx_far, dx_sum, dx_last, kern_own, kern_part,
+    dx, dx_near, dx_half, dx_far, dx_cross, dx_sum, dx_last, kern_own, kern_part,
     dx_send, dx_recv, far_send, far_recv, gw_send, gw_recv, part_send, part_recv,
     kern_send, kern_recv,
 ):
@@ -459,56 +459,36 @@
             {"rows": same_chip},
         )
 
+    def cross_copy():
+        return remote(
+            dx_half.at[:, lanes_of(0)],
+            dx_cross,
+            far_send.at[0, 0],
+            far_recv.at[0, 0],
+            {"hid": part_of(0)},
+        )
+
     def pass_half(i):
         near_copy(0, diagonal, i).wait_recv()
         at = lanes_of(i)
-        dx_half[:, at] = (
-            dx[span(across, tokens), at].astype(jnp.float32) + dx_near[0, :, at].astype(jnp.float32)
-        ).astype(jnp.bfloat16)
-        go(dx_half.at[:, at], dx_far.at[:, at], far_send.at[0, i], far_recv.at[0, i], {"rows": across})
-
-    def inner_column(c, carry):
-        one_column(c, carry)
-
-        @pl.when(c == cols - 1)
-        def _():
-            kern_own[...] = kern[...].astype(jnp.bfloat16)
-            kern_copy.start()
-
-        for a in (1, 0):
-            give(a, c)
-        return carry
-
-    kern_copy = remote(
-        kern_own, kern_part.at[1, 0], kern_send.at[0], kern_recv.at[1, 0], {"crop": 1 - y}
-    )
-    lax.fori_loop(1, 2, inner_column, 0)
-    settle(1, 0)
-    lax.fori_loop(2, cols, inner_column, 0)
-    settle(0, 0)
-    for i in range(depth):
-
-        def one_block(j, carry):
-            g = part_of(i) * per_part + j
-            dx[:, span(g, block)] = token_grad(g)
-            return carry
-
-        lax.fori_loop(0, per_part, one_block, 0)
-        for slot, row in near:
-            near_copy(slot, row, i).start()
-        if i > 0:
-            pass_half(i - 1)
-    pass_half(depth - 1)
+        half_sum = dx[span(across, tokens), at].astype(jnp.float32) + dx_near[0, :, at].astype(jnp.float32)
+        if i == depth - 1:
+            cross_copy().wait_recv()
+            half_sum += dx_cross[...].astype(jnp.float32)
+        dx_half[:, at] = half_sum.astype(jnp.bfloat16)
+        if i == 0:
+            cross_copy().start()
+        else:
+            go(dx_half.at[:, at], dx_far.at[:, at], far_send.at[0, i], far_recv.at[0, i], {"rows": across})
 
     def pass_sum(i):
         at = lanes_of(i)
         near_copy(1, same_chip, i).wait_recv()
-        arrived(dx_far.at[:, at], far_send.at[0, i], far_recv.at[0, i], {"rows": across})
-        dx_sum[i] = (
-            dx[span(r, tokens), at].astype(jnp.float32)
-            + dx_near[1, :, at].astype(jnp.float32)
-            + dx_far[:, at].astype(jnp.float32)
-        ).astype(jnp.bfloat16)
+        own_sum = dx[span(r, tokens), at].astype(jnp.float32) + dx_near[1, :, at].astype(jnp.float32)
+        if i > 0:
+            arrived(dx_far.at[:, at], far_send.at[0, i], far_recv.at[0, i], {"rows": across})
+            own_sum += dx_far[:, at].astype(jnp.float32)
+        dx_sum[i] = own_sum.astype(jnp.bfloat16)
         if i < depth - 1:
             go(
                 dx_sum.at[i],
@@ -518,8 +498,43 @@
                 {"hid": part_of(i)},
             )
 
+    def inner_column(c, carry):
+        one_column(c, carry)
+
+        @pl.when(c == cols - 1)
+        def _():
+            kern_own[...] = kern[...].astype(jnp.bfloat16)
+            kern_copy.start()
+
+        for a in (1, 0):
+            give(a, c)
+        return carry
+
+    kern_copy = remote(
+        kern_own, kern_part.at[1, 0], kern_send.at[0], kern_recv.at[1, 0], {"crop": 1 - y}
+    )
+    lax.fori_loop(1, 2, inner_column, 0)
+    settle(1, 0)
+    lax.fori_loop(2, cols, inner_column, 0)
+    settle(0, 0)
+    for i in range(depth):
+
+        def one_block(j, carry):
+            g = part_of(i) * per_part + j
+            dx[:, span(g, block)] = token_grad(g)
+            return carry
+
+        lax.fori_loop(0, per_part, one_block, 0)
+        for slot, row in near:
+            near_copy(slot, row, i).start()
+        if i > 0:
+            pass_half(i - 1)
+        if i == 1:
+            pass_sum(0)
+    pass_half(depth - 1)
+
     waits = [(a, c) for c in range(1, cols) for a in (1, 0)]
-    sums = list(range(depth))
+    sums = list(range(1, depth))
     while len(waits) > 2:
         settle(*waits.pop(0))
         if sums:
@@ -566,6 +581,7 @@
     for copy in started:
         copy.wait_send()
     kern_copy.wait_send()
+    cross_copy().wait_send()
     for a in range(2):
         for c in range(cols):
             for far in range(2):
@@ -642,6 +658,7 @@
             pltpu.VMEM((2, count, model), bf16),
             pltpu.VMEM((count, model), bf16),
             pltpu.VMEM((count, model), bf16),
+            pltpu.VMEM((count, features), bf16),
             pltpu.VMEM((depth, count, features), bf16),
             pltpu.VMEM((depth - 1, count, features), bf16),
             pltpu.VMEM((16, hidden), bf16),
@@ -812,6 +829,7 @@
             and tokens.shape[0] == 1
             and weight_in.shape[1] % n_rows == 0
             and weight_in.shape[1] >= 2 * n_rows
+            and n_hid >= 2
             and tokens.shape[1] * tokens.shape[2] * n_rows * tokens.shape[3] * n_hid <= 2**22
         )
         chosen = split_hidden if fits else on_device

time: 144 us -> 141 us (0.979)
  Pallas kernels: 143 us -> 140 us
    pallas_call x1, Pallas kernels: 137 us -> 134 us  [split_hidden(): pl.pallas_call(functools.partial(grads_kernel, depth, width, block, cols,...]
where the time goes in v5:
time: 141 us; the launch traced here: 140 us
  Pallas kernels  140 us (99%)
    pallas_call x1, Pallas kernels, split_hidden(): pl.pallas_call(functools.partial(grads_kernel, depth, width, block, cols,...  134 us
    pallas_call x1, Pallas kernels, split_hidden(): pl.pallas_call(functools.partial(finish_kernel, all_cols, nnz), name='fin...  5.73 us

profile of v5, /device:TPU:0, one launch (start us, length us, event | category | flops | bytes accessed | tf_op | source)
XLA Modules:
  0.0 140.5 jit_solution(12941000175540460578)
XLA Ops:
  0.6 134.0 %grads_and_sums.1 = (bf16[128,1024]{1,0:T(8,128)(2,1)}, bf16[2,32,20480]{2,1,0:T(8,128)(2,1)}, f32[16,4096]{1,0:T(8,128)}) custom-call(s32[5,16]{1,0:T(8,128)} %bitcast.20, bf16[128,1024]{1,0:T(8,128)(2,1)} %bitcast.18, bf16[128,1024]{1,0:T(8,128)(2,1)} %bitcast.19, bf16[64,80,256]{2,1,0:T(8,128)(2,1)} %bitcast.16, bf16[64,80,256]{2,1,0:T(8,128)(2,1)} %bitcast.17, ...), custom_call_target="tpu_custom_call" | custom-call | tf_op jit(solution)/shard_map/grads_and_sums/pallas_call | solution.py:625
  134.6 5.7 %finish_weights.1 = (f32[2560,256]{1,0:T(8,128)}, f32[2560,256]{1,0:T(8,128)}, bf16[128,1024]{1,0:T(8,128)(2,1)}, f32[9,4096]{1,0:T(8,128)}) custom-call(bf16[2,32,20480]{2,1,0:T(8,128)(2,1)} %get-tuple-element.11.mine, bf16[128,1024]{1,0:T(8,128)(2,1)} %get-tuple-element.12.dx_mine, f32[16,4096]{1,0:T(8,128)} %get-tuple-element.13.kern_all), custom_call_target="tpu_custom_call" | custom-call | tf_op jit(solution)/shard_map/finish_weights/pallas_call | solution.py:690

commit v6 on v5

--- a/solution.py
+++ b/solution.py
@@ -531,9 +531,10 @@
             pass_half(i - 1)
         if i == 1:
             pass_sum(0)
+
+    settle(1, 1)
     pass_half(depth - 1)
-
-    waits = [(a, c) for c in range(1, cols) for a in (1, 0)]
+    waits = [(a, c) for c in range(1, cols) for a in (1, 0)][1:]
     sums = list(range(1, depth))
     while len(waits) > 2:
         settle(*waits.pop(0))

time: 141 us -> 141 us (level)
  no operation moved by 1% of the time
where the time goes in v6:
time: 141 us; the launch traced here: 140 us
  Pallas kernels  140 us (99%)
    pallas_call x1, Pallas kernels, split_hidden(): pl.pallas_call(functools.partial(grads_kernel, depth, width, block, cols,...  134 us
    pallas_call x1, Pallas kernels, split_hidden(): pl.pallas_call(functools.partial(finish_kernel, all_cols, nnz), name='fin...  5.73 us

profile of v6, /device:TPU:0, one launch (start us, length us, event | category | flops | bytes accessed | tf_op | source)
XLA Modules:
  0.0 140.5 jit_solution(15201477217887363395)
XLA Ops:
  0.6 134.0 %grads_and_sums.1 = (bf16[128,1024]{1,0:T(8,128)(2,1)}, bf16[2,32,20480]{2,1,0:T(8,128)(2,1)}, f32[16,4096]{1,0:T(8,128)}) custom-call(s32[5,16]{1,0:T(8,128)} %bitcast.20, bf16[128,1024]{1,0:T(8,128)(2,1)} %bitcast.18, bf16[128,1024]{1,0:T(8,128)(2,1)} %bitcast.19, bf16[64,80,256]{2,1,0:T(8,128)(2,1)} %bitcast.16, bf16[64,80,256]{2,1,0:T(8,128)(2,1)} %bitcast.17, ...), custom_call_target="tpu_custom_call" | custom-call | tf_op jit(solution)/shard_map/grads_and_sums/pallas_call | solution.py:626
  134.6 5.7 %finish_weights.1 = (f32[2560,256]{1,0:T(8,128)}, f32[2560,256]{1,0:T(8,128)}, bf16[128,1024]{1,0:T(8,128)(2,1)}, f32[9,4096]{1,0:T(8,128)}) custom-call(bf16[2,32,20480]{2,1,0:T(8,128)(2,1)} %get-tuple-element.11.mine, bf16[128,1024]{1,0:T(8,128)(2,1)} %get-tuple-element.12.dx_mine, f32[16,4096]{1,0:T(8,128)} %get-tuple-element.13.kern_all), custom_call_target="tpu_custom_call" | custom-call | tf_op jit(solution)/shard_map/finish_weights/pallas_call | solution.py:691
